TPU v7x, 32 devices: a whole 2x2x4 slice. The times are simulated.
32 devices in a mesh: wide: 8 (over z, y), narrow: 4 (over x, core).
Axes of the slice: x: 2, y: 2, z: 4, core: 2. Of those that a mesh axis runs over, the one named last changes fastest.
Arguments:
- tokens: bfloat16 [64, 600, 768], P(('wide', 'narrow')), may hold values from -6 to 6
- lengths: int32 [64], P(('wide', 'narrow')), may hold values from 256 to 600, as said below
- blocks: int32 [64, 600], P(('wide', 'narrow')), may hold values from 0 to 4, never falling along the last dimension, each value on 1 to 300 neighbouring positions
- ln1_gain: bfloat16 [768], P(('wide', 'narrow')), may hold values from 0.25 to 1.75
- ln1_bias: bfloat16 [768], P(('wide', 'narrow')), may hold values from -1.75 to 1.75
- qkv_weight: bfloat16 [768, 2304], P(('wide', 'narrow')), may hold values from -0.3125 to 0.3125
- qv_bias: bfloat16 [1536], P(('wide', 'narrow')), may hold values from -1.75 to 1.75
- out_weight: bfloat16 [768, 768], P(('wide', 'narrow')), may hold values from -1.25 to 1.25
- out_bias: bfloat16 [768], P(('wide', 'narrow')), may hold values from -1.75 to 1.75
- ln2_gain: bfloat16 [768], P(('wide', 'narrow')), may hold values from 0.25 to 1.75
- ln2_bias: bfloat16 [768], P(('wide', 'narrow')), may hold values from -1.75 to 1.75
- up_weight: bfloat16 [768, 3072], P(('wide', 'narrow')), may hold values from -0.21875 to 0.21875
- up_bias: bfloat16 [3072], P(('wide', 'narrow')), may hold values from -1.75 to 1.75
- down_weight: bfloat16 [3072, 768], P(('wide', 'narrow')), may hold values from -0.109375 to 0.109375
- down_bias: bfloat16 [768], P(('wide', 'narrow')), may hold values from -1.75 to 1.75
- cotangent: bfloat16 [64, 600, 768], P(('wide', 'narrow')), may hold values from -12 to 12
Outputs:
- output: bfloat16 [64, 600, 768], P(('wide', 'narrow'))
- input_grad: float32 [64, 600, 768], P(('wide', 'narrow'))
- ln1_gain_grad: float32 [768], P(('wide', 'narrow'))
- ln1_bias_grad: float32 [768], P(('wide', 'narrow'))
- qkv_weight_grad: float32 [768, 2304], P(('wide', 'narrow'))
- qv_bias_grad: float32 [1536], P(('wide', 'narrow'))
- out_weight_grad: float32 [768, 768], P(('wide', 'narrow'))
- out_bias_grad: float32 [768], P(('wide', 'narrow'))
- ln2_gain_grad: float32 [768], P(('wide', 'narrow'))
- ln2_bias_grad: float32 [768], P(('wide', 'narrow'))
- up_weight_grad: float32 [768, 3072], P(('wide', 'narrow'))
- up_bias_grad: float32 [3072], P(('wide', 'narrow'))
- down_weight_grad: float32 [3072, 768], P(('wide', 'narrow'))
- down_bias_grad: float32 [768], P(('wide', 'narrow'))
Inputs may be any that keep to these rules, and one draw needn't show every extreme that they name: Slots at and after lengths[b] of item b are padding; some item has 600 real tokens and some 256. `blocks`: block ids of an item start at 0 at slot 0 and never fall along the slots.
All inputs are finite; a program needn't handle non-finite values.
Results may differ from a plain program's by a relative error of at most 0.012.
The roundings to bfloat16 on the way count: a program that leaves them out, or rounds other values in their place, can miss the bound.
Values may be sent and summed in bfloat16 or wider, within the bound.
No kernel may reach another device: no remote copies, remote signals or barrier semaphores. Data moves between devices by JAX's collectives and lax.ppermute only.
A program may use at most 256 MiB of HBM per device.

v0:
```python
from functools import partial

import jax
import jax.numpy as jnp
from jax import lax
from jax.sharding import PartitionSpec as P

D = 768
HEADS = 12
HEAD = 64


norm_epsilon = 1e-05
masked_score = -1e30


def layer_norm(values, gain, shift):
    centred = values - jnp.mean(values, axis=-1, keepdims=True)
    inverse = lax.rsqrt(jnp.mean(centred * centred, axis=-1, keepdims=True) + norm_epsilon)
    scaled = centred * inverse
    return (scaled * gain + shift, scaled, inverse)


def norm_back(d_normed, scaled, inverse, gain):
    gain_grad = jnp.sum(d_normed * scaled, axis=0)
    shift_grad = jnp.sum(d_normed, axis=0)
    d_scaled = d_normed * gain
    centre_term = jnp.mean(d_scaled, axis=-1, keepdims=True)
    slope_term = jnp.mean(d_scaled * scaled, axis=-1, keepdims=True)
    return (inverse * (d_scaled - centre_term - scaled * slope_term), gain_grad, shift_grad)


def allowed_pairs(item_length, block_ids):
    slot_count = block_ids.shape[0]
    column = lax.broadcasted_iota(jnp.int32, (slot_count, slot_count), 1)
    return (block_ids[None, :] <= block_ids[:, None]) & (column < item_length)


def head_split(packed, index):
    slot_count = packed.shape[0]
    return packed[:, index * D : (index + 1) * D].reshape(slot_count, HEADS, HEAD)


def score_table(queries, key_rows, allowed):
    scores = jnp.einsum(
        "qhd,khd->hqk", queries, key_rows, preferred_element_type=jnp.float32
    ) * HEAD ** (-0.5)
    return jnp.where(allowed[None], scores, masked_score)


def attend_forward(packed):
    qkv_item, item_length, block_ids = packed
    slot_count = qkv_item.shape[0]
    scores = score_table(
        head_split(qkv_item, 0), head_split(qkv_item, 1), allowed_pairs(item_length, block_ids)
    )
    peak_score = jnp.max(scores, axis=-1, keepdims=True)
    exponent = jnp.exp(scores - peak_score)
    row_total = jnp.sum(exponent, axis=-1, keepdims=True)
    probs_low = (exponent / row_total).astype(jnp.bfloat16)
    mixed_heads = jnp.einsum(
        "hqk,khd->qhd", probs_low, head_split(qkv_item, 2), preferred_element_type=jnp.float32
    )
    return (
        mixed_heads.reshape(slot_count, D).astype(jnp.bfloat16),
        peak_score + jnp.log(row_total),
    )


def attend_backward(packed):
    qkv_item, item_length, block_ids, log_total, d_mixed = packed
    slot_count = qkv_item.shape[0]
    queries = head_split(qkv_item, 0)
    key_rows = head_split(qkv_item, 1)
    value_rows = head_split(qkv_item, 2)
    scores = score_table(queries, key_rows, allowed_pairs(item_length, block_ids))
    probs = jnp.exp(scores - log_total)
    probs_low = probs.astype(jnp.bfloat16)
    d_heads = d_mixed.reshape(slot_count, HEADS, HEAD)
    d_values = jnp.einsum("hqk,qhd->khd", probs_low, d_heads, preferred_element_type=jnp.float32)
    d_probs = jnp.einsum("qhd,khd->hqk", d_heads, value_rows, preferred_element_type=jnp.float32)
    d_scores = (probs * (d_probs - jnp.sum(probs * d_probs, axis=-1, keepdims=True))).astype(
        jnp.bfloat16
    )
    d_queries = jnp.einsum(
        "hqk,khd->qhd", d_scores, key_rows, preferred_element_type=jnp.float32
    ) * HEAD ** (-0.5)
    d_keys = jnp.einsum(
        "hqk,qhd->khd", d_scores, queries, preferred_element_type=jnp.float32
    ) * HEAD ** (-0.5)
    joined = jnp.concatenate(
        [
            d_queries.reshape(slot_count, D),
            d_keys.reshape(slot_count, D),
            d_values.reshape(slot_count, D),
        ],
        axis=1,
    )
    return joined.astype(jnp.bfloat16)


def fetch(shards):
    (
        gain_one,
        shift_one,
        w_qkv,
        bias_qv,
        w_out,
        bias_out,
        gain_two,
        shift_two,
        w_up,
        bias_up,
        w_down,
        bias_down,
    ) = shards
    whole_set = (
        lax.all_gather(gain_one, ("wide", "narrow"), axis=0, tiled=True),
        lax.all_gather(shift_one, ("wide", "narrow"), axis=0, tiled=True),
        lax.all_gather(w_qkv, ("wide", "narrow"), axis=0, tiled=True),
        lax.all_gather(bias_qv, ("wide", "narrow"), axis=0, tiled=True),
        lax.all_gather(w_out, ("wide", "narrow"), axis=0, tiled=True),
        lax.all_gather(bias_out, ("wide", "narrow"), axis=0, tiled=True),
        lax.all_gather(gain_two, ("wide", "narrow"), axis=0, tiled=True),
        lax.all_gather(shift_two, ("wide", "narrow"), axis=0, tiled=True),
        lax.all_gather(w_up, ("wide", "narrow"), axis=0, tiled=True),
        lax.all_gather(bias_up, ("wide", "narrow"), axis=0, tiled=True),
        lax.all_gather(w_down, ("wide", "narrow"), axis=0, tiled=True),
        lax.all_gather(bias_down, ("wide", "narrow"), axis=0, tiled=True),
    )
    return whole_set


def reduce_grads(grads):
    (
        gain_one,
        shift_one,
        w_qkv,
        bias_qv,
        w_out,
        bias_out,
        gain_two,
        shift_two,
        w_up,
        bias_up,
        w_down,
        bias_down,
    ) = grads
    owned = (
        lax.psum_scatter(gain_one, ("wide", "narrow"), scatter_dimension=0, tiled=True),
        lax.psum_scatter(shift_one, ("wide", "narrow"), scatter_dimension=0, tiled=True),
        lax.psum_scatter(w_qkv, ("wide", "narrow"), scatter_dimension=0, tiled=True),
        lax.psum_scatter(bias_qv, ("wide", "narrow"), scatter_dimension=0, tiled=True),
        lax.psum_scatter(w_out, ("wide", "narrow"), scatter_dimension=0, tiled=True),
        lax.psum_scatter(bias_out, ("wide", "narrow"), scatter_dimension=0, tiled=True),
        lax.psum_scatter(gain_two, ("wide", "narrow"), scatter_dimension=0, tiled=True),
        lax.psum_scatter(shift_two, ("wide", "narrow"), scatter_dimension=0, tiled=True),
        lax.psum_scatter(w_up, ("wide", "narrow"), scatter_dimension=0, tiled=True),
        lax.psum_scatter(bias_up, ("wide", "narrow"), scatter_dimension=0, tiled=True),
        lax.psum_scatter(w_down, ("wide", "narrow"), scatter_dimension=0, tiled=True),
        lax.psum_scatter(bias_down, ("wide", "narrow"), scatter_dimension=0, tiled=True),
    )
    return tuple(owned)


def body(
    tokens,
    lengths,
    blocks,
    ln1_gain,
    ln1_bias,
    qkv_weight,
    qv_bias,
    out_weight,
    out_bias,
    ln2_gain,
    ln2_bias,
    up_weight,
    up_bias,
    down_weight,
    down_bias,
    cotangent,
):
    item_count, slot_count, model_width = tokens.shape
    row_count = item_count * slot_count
    shards = (
        ln1_gain,
        ln1_bias,
        qkv_weight,
        qv_bias,
        out_weight,
        out_bias,
        ln2_gain,
        ln2_bias,
        up_weight,
        up_bias,
        down_weight,
        down_bias,
    )
    layer_weights = fetch(shards)
    (
        gain_one,
        shift_one,
        w_qkv,
        bias_qv,
        w_out,
        bias_out,
        gain_two,
        shift_two,
        w_up,
        bias_up,
        w_down,
        bias_down,
    ) = layer_weights
    inputs = tokens.reshape(row_count, model_width).astype(jnp.float32)
    normed_one, scaled_one, inverse_one = layer_norm(
        inputs, gain_one.astype(jnp.float32), shift_one.astype(jnp.float32)
    )
    normed_one = normed_one.astype(jnp.bfloat16)
    qv_float = bias_qv.astype(jnp.float32)
    bias_full = jnp.concatenate(
        [qv_float[:model_width], jnp.zeros((model_width,), jnp.float32), qv_float[model_width:]]
    )
    qkv_low = (jnp.dot(normed_one, w_qkv, preferred_element_type=jnp.float32) + bias_full).astype(
        jnp.bfloat16
    )
    qkv_items = qkv_low.reshape(item_count, slot_count, 3 * model_width)
    mixed_items, log_totals = lax.map(attend_forward, (qkv_items, lengths, blocks))
    mixed_low = mixed_items.reshape(row_count, model_width)
    middle = (
        inputs
        + jnp.dot(mixed_low, w_out, preferred_element_type=jnp.float32)
        + bias_out.astype(jnp.float32)
    )
    normed_two, scaled_two, inverse_two = layer_norm(
        middle, gain_two.astype(jnp.float32), shift_two.astype(jnp.float32)
    )
    normed_two = normed_two.astype(jnp.bfloat16)
    pre_active = jnp.dot(normed_two, w_up, preferred_element_type=jnp.float32) + bias_up.astype(
        jnp.float32
    )
    active, gelu_back = jax.vjp(partial(jax.nn.gelu, approximate=True), pre_active)
    active_low = active.astype(jnp.bfloat16)
    branch_mlp = jnp.dot(active_low, w_down, preferred_element_type=jnp.float32) + bias_down.astype(
        jnp.float32
    )
    slot_ids = lax.broadcasted_iota(jnp.int32, (item_count, slot_count), 1)
    valid_rows = (slot_ids < lengths[:, None]).astype(jnp.float32).reshape(row_count, 1)
    output = (
        ((middle + branch_mlp) * valid_rows)
        .astype(jnp.bfloat16)
        .reshape(item_count, slot_count, model_width)
    )
    back_weights = fetch(shards)
    (
        back_gain_one,
        back_shift_one,
        back_qkv,
        back_bias_qv,
        back_out,
        back_bias_out,
        back_gain_two,
        back_shift_two,
        back_up,
        back_bias_up,
        back_down,
        back_bias_down,
    ) = back_weights
    d_result = cotangent.reshape(row_count, model_width).astype(jnp.float32) * valid_rows
    d_lower = d_result.astype(jnp.bfloat16)
    grad_bias_down = jnp.sum(d_lower.astype(jnp.float32), axis=0)
    grad_down = jnp.einsum("rf,rd->fd", active_low, d_lower, preferred_element_type=jnp.float32)
    d_active = jnp.einsum("rd,fd->rf", d_lower, back_down, preferred_element_type=jnp.float32)
    d_pre = gelu_back(d_active)[0].astype(jnp.bfloat16)
    grad_bias_up = jnp.sum(d_pre.astype(jnp.float32), axis=0)
    grad_up = jnp.einsum("rd,rf->df", normed_two, d_pre, preferred_element_type=jnp.float32)
    d_normed_two = jnp.einsum("rf,df->rd", d_pre, back_up, preferred_element_type=jnp.float32)
    d_inner, grad_gain_two, grad_shift_two = norm_back(
        d_normed_two, scaled_two, inverse_two, back_gain_two.astype(jnp.float32)
    )
    d_middle = d_result + d_inner
    d_branch = d_middle.astype(jnp.bfloat16)
    grad_bias_out = jnp.sum(d_branch.astype(jnp.float32), axis=0)
    grad_out = jnp.einsum("rd,re->de", mixed_low, d_branch, preferred_element_type=jnp.float32)
    d_mixed = jnp.einsum(
        "re,de->rd", d_branch, back_out, preferred_element_type=jnp.float32
    ).astype(jnp.bfloat16)
    d_qkv = lax.map(
        attend_backward,
        (
            qkv_items,
            lengths,
            blocks,
            log_totals,
            d_mixed.reshape(item_count, slot_count, model_width),
        ),
    )
    d_qkv = d_qkv.reshape(row_count, 3 * model_width)
    column_sums = jnp.sum(d_qkv.astype(jnp.float32), axis=0)
    grad_bias_qv = jnp.concatenate([column_sums[:model_width], column_sums[2 * model_width :]])
    grad_qkv = jnp.einsum("rd,re->de", normed_one, d_qkv, preferred_element_type=jnp.float32)
    d_normed_one = jnp.einsum("re,de->rd", d_qkv, back_qkv, preferred_element_type=jnp.float32)
    d_first, grad_gain_one, grad_shift_one = norm_back(
        d_normed_one, scaled_one, inverse_one, back_gain_one.astype(jnp.float32)
    )
    input_grad = (d_middle + d_first).reshape(item_count, slot_count, model_width)
    owned = reduce_grads(
        (
            grad_gain_one,
            grad_shift_one,
            grad_qkv,
            grad_bias_qv,
            grad_out,
            grad_bias_out,
            grad_gain_two,
            grad_shift_two,
            grad_up,
            grad_bias_up,
            grad_down,
            grad_bias_down,
        )
    )
    return (output, input_grad) + owned


def solution(mesh):
    return jax.shard_map(
        body,
        mesh=mesh,
        in_specs=(
            P(("wide", "narrow"), None, None),
            P(("wide", "narrow")),
            P(("wide", "narrow"), None),
            P(("wide", "narrow")),
            P(("wide", "narrow")),
            P(("wide", "narrow"), None),
            P(("wide", "narrow")),
            P(("wide", "narrow"), None),
            P(("wide", "narrow")),
            P(("wide", "narrow")),
            P(("wide", "narrow")),
            P(("wide", "narrow"), None),
            P(("wide", "narrow")),
            P(("wide", "narrow"), None),
            P(("wide", "narrow")),
            P(("wide", "narrow"), None, None),
        ),
        out_specs=(
            P(("wide", "narrow"), None, None),
            P(("wide", "narrow"), None, None),
            P(("wide", "narrow")),
            P(("wide", "narrow")),
            P(("wide", "narrow"), None),
            P(("wide", "narrow")),
            P(("wide", "narrow"), None),
            P(("wide", "narrow")),
            P(("wide", "narrow")),
            P(("wide", "narrow")),
            P(("wide", "narrow"), None),
            P(("wide", "narrow")),
            P(("wide", "narrow"), None),
            P(("wide", "narrow")),
        ),
        check_vma=False,
    )
```

profile of v0, /device:TPU:0, one launch (start us, length us, event | category | flops | bytes accessed | tf_op | source)
XLA Modules:
  0.0 839.5 jit_solution(17000271752070816200)
XLA Ops:
  10.1 2.0 convert_reduce_fusion.4
  12.1 2.2 multiply_reduce_fusion.6
  16.5 42.7 %all-reduce.17 = (bf16[1536]{0:T(1024)(128)(2,1)S(1)}, bf16[768]{0:T(1024)(128)(2,1)S(1)}, bf16[768]{0:T(1024)(128)(2,1)S(1)}, bf16[768]{0:T(1024)(128)(2,1)S(1)...) all-reduce(bf16[1536]{0:T(1024)(128)(2,1)S(1)} %dynamic-update-slic, ...), channel_id=1, replica_groups=mesh['wide'=8,'narrow'=4] {'wide','narrow'}, use_global_device_ids=true, to_apply=%add.2 | all-reduce | flops 9216 | bytes 36864
  61.7 3.2 fusion.27
  64.9 2.4 fusion.26
  67.3 6.6 all-gather.5.cloned.1.call-done
  73.9 10.0 %fusion.22 = bf16[1200,2304]{1,0:T(8,128)(2,1)} fusion(bf16[768,2304]{1,0:T(8,128)(2,1)} %all-gather.5.cloned.1.call-done, f32[2304]{0:T(1024)S(1)} %pad_maximum_fusion, f32[1200,768]{1,0:T(8,128)} %fusion.26, f32[768]{0:T(1024)S(1)} %convert_element_type.143, f32[768]{0:T(1024)S(1)} %convert_element_type.142), kind=kOutput, calls=%fused_computation.47 | convolution fusion | flops 4255027200 | bytes 12770304 | tf_op jit(solution)/shard_map/dot_general | solution.py:224
  84.0 8.8 %copy.52 = bf16[2,600,2304]{1,2,0:T(8,128)(2,1)} copy(bf16[2,600,2304]{2,1,0:T(8,128)(2,1)} %bitcast.156) | data formatting | bytes 11059200 | tf_op jit(solution)/shard_map/while | solution.py:228
  92.8 78.2 %while.22 = (s32[]{:T(128)}, bf16[2,600,768]{2,1,0:T(8,128)(2,1)}, f32[2,12,600,1]{2,1,3,0:T(8,128)S(1)}, bf16[2,600,2304]{1,2,0:T(8,128)(2,1)}, s32[2,600]{1,0:T(2,128)S(1)}, /*index=5*/s32[2]{0:T(128)S(1)}, s32[]{:T(128)}) while((s32[]{:T(128)}, bf16[2,600,768]{2,1,0:T(8,128)(2,1)}, f32[2,12,600,1]{2,1,3,0:T(8,128)S(1)}, ...), condition=%wide.region_5.6_spmd, body=%wide.region_2.5_spmd.sunk | while | flops 1158934144 | bytes 71987392 | solution.py:228
  94.6 2.1 dynamic-slice_bitcast_fusion.6
  96.6 1.2 fusion.98
  97.9 8.2 fusion.99
  106.0 10.1 %fusion.100 = f32[12,600]{1,0:T(8,128)S(1)} fusion(f32[12,600,600]{1,2,0:T(8,128)} %get-tuple-element.288, f32[12,600]{1,0:T(8,128)S(1)} %get-tuple-element.289, pred[600,600]{0,1:T(8,128)(4,1)S(1)} %compare_and_fusion.4), kind=kLoop, calls=%fused_computation.4.clone.1 | loop fusion | flops 17272800 | bytes 17697600 | tf_op jit(solution)/shard_map/while/body/eval_jaxpr/reduce_sum | solution.py:59
  116.2 13.0 %fusion.101 = bf16[12,64,600]{2,1,0:T(8,128)(2,1)} fusion(bf16[600,12,64]{0,2,1:T(8,128)(2,1)} %bitcast.152, f32[12,600,600]{1,2,0:T(8,128)} %get-tuple-element.288, f32[12,600]{1,0:T(8,128)S(1)} %fusion.100, f32[12,600]{1,0:T(8,128)S(1)} %get-tuple-element.289, pred[600,600]{0,1:T(8,128)(4,1)S(1)} %compare_and_fusion.4), kind=kOutput, calls=%fused_computation.8.clone.1 | convolution fusion | flops 575020800 | bytes 19540800 | tf_op jit(solution)/shard_map/while/body/eval_jaxpr/hqk,khd->qhd/dot_general | solution.py:61
  129.1 1.6 copy.68
  130.7 1.0 constant_dynamic-update-slice_fusion.2
  133.3 2.1 dynamic-slice_bitcast_fusion.6
  135.4 1.2 fusion.98
  136.6 8.2 fusion.99
  144.8 10.1 %fusion.100 = f32[12,600]{1,0:T(8,128)S(1)} fusion(f32[12,600,600]{1,2,0:T(8,128)} %get-tuple-element.288, f32[12,600]{1,0:T(8,128)S(1)} %get-tuple-element.289, pred[600,600]{0,1:T(8,128)(4,1)S(1)} %compare_and_fusion.4), kind=kLoop, calls=%fused_computation.4.clone.1 | loop fusion | flops 17272800 | bytes 17697600 | tf_op jit(solution)/shard_map/while/body/eval_jaxpr/reduce_sum | solution.py:59
  154.9 13.1 %fusion.101 = bf16[12,64,600]{2,1,0:T(8,128)(2,1)} fusion(bf16[600,12,64]{0,2,1:T(8,128)(2,1)} %bitcast.152, f32[12,600,600]{1,2,0:T(8,128)} %get-tuple-element.288, f32[12,600]{1,0:T(8,128)S(1)} %fusion.100, f32[12,600]{1,0:T(8,128)S(1)} %get-tuple-element.289, pred[600,600]{0,1:T(8,128)(4,1)S(1)} %compare_and_fusion.4), kind=kOutput, calls=%fused_computation.8.clone.1 | convolution fusion | flops 575020800 | bytes 19540800 | tf_op jit(solution)/shard_map/while/body/eval_jaxpr/hqk,khd->qhd/dot_general | solution.py:61
  168.0 1.6 copy.68
  171.0 3.7 fusion.45
  174.8 1.8 copy-done.5
  177.2 18.0 %all-gather.9.cloned.1.call-done = bf16[768,3072]{1,0:T(8,128)(2,1)} async-done(((bf16[24,3072]{1,0:T(8,128)(2,1)}), bf16[768,3072]{1,0:T(8,128)(2,1)}) %all-gather.9.cloned.1.call-update) | async-done | bytes 4718608 | tf_op jit(solution)/shard_map/all_gather | solution.py:126
  195.2 12.4 %convolution_add_fusion.1 = f32[1200,3072]{1,0:T(8,128)} fusion(bf16[768,3072]{1,0:T(8,128)(2,1)} %all-gather.9.cloned.1.call-done, f32[3072]{0:T(1024)S(1)} %copy-done.35, f32[1200,768]{1,0:T(8,128)} %copy-done.5, f32[768]{0:T(1024)S(1)} %copy-done.37, f32[768]{0:T(1024)S(1)} %copy-done.32, f32[1200]{0:T(1024)S(1)} %add_rsqrt_fusion, ...), kind=kOutput, calls=%fused_computation.45 | convolution fusion | flops 5670604800 | bytes 23178624 | tf_op jit(solution)/shard_map/dot_general | solution.py:239
  207.5 52.9 %all-gather.11.cloned.1.call-done = bf16[3072,768]{1,0:T(8,128)(2,1)} async-done(((bf16[96,768]{1,0:T(8,128)(2,1)}), bf16[3072,768]{1,0:T(8,128)(2,1)}) %all-gather.11.cloned.1.call-update) | async-done | bytes 4718608 | tf_op jit(solution)/shard_map/all_gather | solution.py:128
  260.4 18.6 %convert_reduce_fusion = (f32[3072]{0:T(1024)}, bf16[1200,3072]{1,0:T(8,128)(2,1)}) fusion(f32[1200,3072]{1,0:T(8,128)} %convolution_add_fusion.1, bf16[1200,768]{1,0:T(8,128)(2,1)S(1)} %copy-done.10, bf16[3072,768]{1,0:T(8,128)(2,1)} %all-gather.11.cloned.1.call-done), kind=kOutput, calls=%fused_computation.42 | convolution fusion | flops 5743408128 | bytes 28692480 | tf_op jit(solution)/shard_map/rd,fd->rf/dot_general | solution.py:273
  279.0 10.6 %multiply_reduce_fusion.1 = (f32[768]{0:T(1024)}, f32[1200]{0:T(1024)S(1)}, f32[1200]{0:T(1024)S(1)}, f32[768]{0:T(1024)}, f32[1200,768]{1,0:T(8,128)S(1)}) fusion(f32[1200,768]{1,0:T(8,128)S(1)} %copy-done.6, f32[1200]{0:T(1024)S(1)} %add_rsqrt_fusion, f32[1200]{0:T(1024)S(1)} %broadcast_multiply_fusion.4, f32[768]{0:T(1024)S(1)} %copy-done.32, ...), kind=kOutput, calls=%fused_computation.59 | convolution fusion | flops 5670600704 | bytes 19492608 | tf_op jit(solution)/shard_map/rf,df->rd/dot_general | solution.py:277
  289.7 2.3 convert_reduce_fusion.3
  292.0 1.9 copy-done.8
  293.9 3.2 fusion.35
  297.2 4.9 convolution_convert_fusion
  302.1 116.0 %while.23 = (s32[]{:T(128)}, bf16[2,600,2304]{1,2,0:T(8,128)(2,1)}, bf16[2,600,2304]{1,2,0:T(8,128)(2,1)}, s32[2,600]{1,0:T(2,128)S(1)}, s32[2]{0:T(128)S(1)}, /...) while((s32[]{:T(128)}, bf16[2,600,2304]{1,2,0:T(8,128)(2,1)}, ...), condition=%wide.region_12.13_spmd, body=%wide.region_10.12_spmd.sunk | while | flops 2840911872 | bytes 160925648 | solution.py:288
  303.9 1.3 constant_dynamic-slice_fusion.2
  305.8 2.1 dynamic-slice_bitcast_fusion.7
  308.3 8.2 fusion.113
  316.4 11.0 %fusion.114 = bf16[12,64,600]{2,1,0:T(8,128)(2,1)S(1)} fusion(bf16[600,12,64]{0,2,1:T(8,128)(2,1)S(1)} %bitcast.148, f32[12,600,600]{1,2,0:T(8,128)} %fusion.113, f32[12,600]{1,0:T(8,128)S(1)} %dynamic-slice_bitcast_fusion.8, pred[600,600]{0,1:T(8,128)(4,1)S(1)} %compare_and_fusion.5), kind=kOutput, calls=%fused_computation.26.clone.1 | convolution fusion | flops 570700800 | bytes 19512000 | tf_op jit(solution)/shard_map/while/body/eval_jaxpr/hqk,qhd->khd/dot_general | solution.py:80
  327.4 13.2 %multiply_reduce_fusion.10 = (f32[12,600]{1,0:T(8,128)S(1)}, f32[12,600,600]{1,2,0:T(8,128)}) fusion(f32[12,600,600]{1,2,0:T(8,128)} %fusion.113, f32[12,600]{1,0:T(8,128)S(1)} %dynamic-slice_bitcast_fusion.8, pred[600,600]{0,1:T(8,128)(4,1)S(1)} %compare_and_fusion.5, bf16[600,12,64]{0,2,1:T(8,128)(2,1)S(1)} %bitcast.149, ...), kind=kOutput, calls=%fused_computation.16.clone.1 | convolution fusion | flops 574552832 | bytes 36820800 | tf_op jit(solution)/shard_map/while/body/eval_jaxpr/qhd,khd->hqk/dot_general | solution.py:81
  340.7 13.4 %multiply_convert_fusion.10 = bf16[12,600,600]{1,2,0:T(8,128)(2,1)S(1)} fusion(f32[12,600,600]{1,2,0:T(8,128)} %get-tuple-element.300, f32[12,600,600]{1,2,0:T(8,128)} %fusion.113, f32[12,600]{1,0:T(8,128)S(1)} %get-tuple-element.301, f32[12,600]{1,0:T(8,128)S(1)} %dynamic-slice_bitcast_fusion.8, pred[600,600]{0,1:T(8,128)(4,1)S(1)} %compare_and_fusion.5), kind=kLoop, calls=%fused_computation.15.clone.1 | loop fusion | flops 25920000 | bytes 43617600 | tf_op jit(solution)/shard_map/while/body/eval_jaxpr/convert_element_type | solution.py:82
  354.1 1.7 multiply_convert_fusion.12
  355.8 2.8 multiply_convert_fusion.11
  358.6 1.9 maximum_dynamic-update-slice_fusion.2
  362.1 1.2 constant_dynamic-slice_fusion.2
  364.0 2.1 dynamic-slice_bitcast_fusion.7
  366.4 8.1 fusion.113
  374.5 10.8 %fusion.114 = bf16[12,64,600]{2,1,0:T(8,128)(2,1)S(1)} fusion(bf16[600,12,64]{0,2,1:T(8,128)(2,1)S(1)} %bitcast.148, f32[12,600,600]{1,2,0:T(8,128)} %fusion.113, f32[12,600]{1,0:T(8,128)S(1)} %dynamic-slice_bitcast_fusion.8, pred[600,600]{0,1:T(8,128)(4,1)S(1)} %compare_and_fusion.5), kind=kOutput, calls=%fused_computation.26.clone.1 | convolution fusion | flops 570700800 | bytes 19512000 | tf_op jit(solution)/shard_map/while/body/eval_jaxpr/hqk,qhd->khd/dot_general | solution.py:80
  385.3 13.1 %multiply_reduce_fusion.10 = (f32[12,600]{1,0:T(8,128)S(1)}, f32[12,600,600]{1,2,0:T(8,128)}) fusion(f32[12,600,600]{1,2,0:T(8,128)} %fusion.113, f32[12,600]{1,0:T(8,128)S(1)} %dynamic-slice_bitcast_fusion.8, pred[600,600]{0,1:T(8,128)(4,1)S(1)} %compare_and_fusion.5, bf16[600,12,64]{0,2,1:T(8,128)(2,1)S(1)} %bitcast.149, ...), kind=kOutput, calls=%fused_computation.16.clone.1 | convolution fusion | flops 574552832 | bytes 36820800 | tf_op jit(solution)/shard_map/while/body/eval_jaxpr/qhd,khd->hqk/dot_general | solution.py:81
  398.5 13.0 %multiply_convert_fusion.10 = bf16[12,600,600]{1,2,0:T(8,128)(2,1)S(1)} fusion(f32[12,600,600]{1,2,0:T(8,128)} %get-tuple-element.300, f32[12,600,600]{1,2,0:T(8,128)} %fusion.113, f32[12,600]{1,0:T(8,128)S(1)} %get-tuple-element.301, f32[12,600]{1,0:T(8,128)S(1)} %dynamic-slice_bitcast_fusion.8, pred[600,600]{0,1:T(8,128)(4,1)S(1)} %compare_and_fusion.5), kind=kLoop, calls=%fused_computation.15.clone.1 | loop fusion | flops 25920000 | bytes 43617600 | tf_op jit(solution)/shard_map/while/body/eval_jaxpr/convert_element_type | solution.py:82
  411.5 1.7 multiply_convert_fusion.12
  413.2 2.8 multiply_convert_fusion.11
  416.0 1.9 maximum_dynamic-update-slice_fusion.2
  418.2 11.7 %convolution_bitcast_fusion = f32[768,2304]{1,0:T(8,128)} fusion(bf16[2,600,2304]{1,2,0:T(8,128)(2,1)} %get-tuple-element.86, bf16[2,600,768]{2,1,0:T(8,128)(2,1)} %param.20, f32[768]{0:T(1024)S(1)} %copy-done.40, f32[768]{0:T(1024)S(1)} %copy-done.31, f32[2,600]{1,0:T(2,128)S(1)} %copy-done.29, f32[2,600]{1,0:T(2,128)S(1)} %copy-done.25), kind=kOutput, calls=%fused_computation.48 | convolution fusion | flops 4252262400 | bytes 14466432 | tf_op jit(solution)/shard_map/rd,re->de/dot_general | solution.py:301
  429.9 1.4 copy-done.11
  431.4 13.5 %fusion.39 = f32[3072,768]{1,0:T(8,128)} fusion(bf16[1200,768]{1,0:T(8,128)(2,1)S(1)} %copy-done.11, f32[1200,3072]{1,0:T(8,128)} %convolution_add_fusion.1), kind=kOutput, calls=%fused_computation.99 | convolution fusion | flops 5695488000 | bytes 26025984 | tf_op jit(solution)/shard_map/rf,rd->fd/dot_general | solution.py:272
  445.6 13.2 %fusion.38 = f32[768,3072]{1,0:T(8,128)} fusion(bf16[1200,3072]{1,0:T(8,128)(2,1)} %get-tuple-element.199, f32[1200,768]{1,0:T(8,128)} %copy-done.5, f32[768]{0:T(1024)S(1)} %copy-done.38, f32[768]{0:T(1024)S(1)} %copy-done.33, f32[1200]{0:T(1024)S(1)} %copy-done.27, f32[1200]{0:T(1024)S(1)} %copy-done.14), kind=kOutput, calls=%fused_computation.98 | convolution fusion | flops 5666918400 | bytes 20512128 | tf_op jit(solution)/shard_map/rd,rf->df/dot_general | solution.py:276
  460.9 9.0 %copy.56 = bf16[2,600,2304]{2,1,0:T(8,128)(2,1)} copy(bf16[2,600,2304]{1,2,0:T(8,128)(2,1)} %get-tuple-element.86) | data formatting | bytes 11059200 | tf_op jit(solution)/shard_map/while | solution.py:288
  469.8 3.8 convert_reduce_fusion.1
  474.2 10.7 %fusion.40 = (f32[768]{0:T(1024)S(1)}, f32[768]{0:T(1024)S(1)}, f32[1200]{0:T(1024)S(1)}, f32[1200]{0:T(1024)S(1)}, f32[1200,768]{1,0:T(8,128)}) fusion(f32[1200]{0:T(1024)S(1)} %copy-done.21, f32[1200]{0:T(1024)S(1)} %copy-done.16, bf16[2,600,768]{2,1,0:T(8,128)(2,1)S(1)} %copy-done.2, f32[1200,768]{1,0:T(8,128)S(1)} %copy-done.9, ...), kind=kOutput, calls=%fused_computation.100 | convolution fusion | flops 4255944704 | bytes 18312960 | tf_op jit(solution)/shard_map/re,de->rd/dot_general | solution.py:302
  484.9 42.1 %all-reduce.16 = (f32[768]{0:T(1024)S(1)}, f32[768]{0:T(1024)S(1)}, f32[1536]{0:T(1024)S(1)}, f32[768]{0:T(1024)S(1)}, f32[768]{0:T(1024)S(1)}, /*index=5*/f32[7...) all-reduce(f32[768]{0:T(1024)S(1)} %get-tuple-element.133, ...), channel_id=2, replica_groups=mesh['wide'=8,'narrow'=4] {'wide','narrow'}, use_global_device_ids=true, to_apply=%region_16.17.clone | all-reduce | flops 9216 | bytes 73728
  531.8 5.2 multiply_add_fusion
  537.0 14.2 %fusion.28 = bf16[1200,768]{1,0:T(8,128)(2,1)} fusion(f32[1200,768]{1,0:T(8,128)S(1)} %copy-done.7, bf16[3072,768]{1,0:T(8,128)(2,1)} %all-gather.11.cloned.1.call-done, f32[1200]{0:T(1024)S(1)} %copy-done.19, f32[768]{0:T(1024)S(1)} %convert_element_type.153, f32[1200,3072]{1,0:T(8,128)} %convolution_add_fusion.1), kind=kOutput, calls=%fused_computation.75 | convolution fusion | flops 5699174400 | bytes 25001664 | tf_op jit(solution)/shard_map/dot_general | solution.py:244
  551.2 139.2 %reduce-scatter.11.cloned.1.call-done = f32[96,768]{1,0:T(8,128)} async-done(((f32[3072,768]{1,0:T(8,128)}), f32[96,768]{1,0:T(8,128)}) %reduce-scatter.11.cloned.1.call-update) | async-done | bytes 294928 | tf_op jit(solution)/shard_map/reduce_scatter | solution.py:160
  690.4 142.1 %reduce-scatter.9.cloned.1.call-done = f32[24,3072]{1,0:T(8,128)} async-done(((f32[768,3072]{1,0:T(8,128)}), f32[24,3072]{1,0:T(8,128)}) %reduce-scatter.9.cloned.1.call-update) | async-done | bytes 294928 | tf_op jit(solution)/shard_map/reduce_scatter | solution.py:158
  (207 shorter events, 25.4 us)
Async XLA Ops:
  7.2 7.2 copy-start.45
  7.2 7.4 copy-start.49
  7.2 7.7 copy-start.50
  7.2 7.9 copy-start.51
  7.2 8.1 copy-start.52
  7.2 8.3 copy-start.53
  7.2 8.6 %copy-start.54 = (bf16[24]{0:T(256)(128)(2,1)S(1)}, bf16[24]{0:T(256)(128)(2,1)}, u32[]{:S(2)}) copy-start(bf16[24]{0:T(256)(128)(2,1)} %param.29) | copy-start | bytes 148
  7.3 8.8 %copy-start.55 = (bf16[48]{0:T(256)(128)(2,1)S(1)}, bf16[48]{0:T(256)(128)(2,1)}, u32[]{:S(2)}) copy-start(bf16[48]{0:T(256)(128)(2,1)} %param.26) | copy-start | bytes 292
  7.3 9.0 %copy-start.56 = (bf16[96]{0:T(256)(128)(2,1)S(1)}, bf16[96]{0:T(256)(128)(2,1)}, u32[]{:S(2)}) copy-start(bf16[96]{0:T(256)(128)(2,1)} %param.32) | copy-start | bytes 580
  7.3 66.6 %all-gather.5.cloned.1.call-start = ((), (), s32[]{:S(2)}) async-start(), calls=%async_computation.4 | async-start | bytes 3649536 | tf_op jit(solution)/shard_map/all_gather | solution.py:120
  8.0 163.0 %all-gather.7.cloned.1.call-start = ((), (), s32[]{:S(2)}) async-start(), calls=%async_computation.5 | async-start | bytes 1216512 | tf_op jit(solution)/shard_map/all_gather | solution.py:122
  8.8 186.4 %all-gather.9.cloned.1.call-start = ((), (), s32[]{:S(2)}) async-start(), calls=%async_computation.6 | async-start | bytes 4866048 | tf_op jit(solution)/shard_map/all_gather | solution.py:126
  9.5 250.9 %all-gather.11.cloned.1.call-start = ((), (), s32[]{:S(2)}) async-start(), calls=%async_computation.7 | async-start | bytes 4866048 | tf_op jit(solution)/shard_map/all_gather | solution.py:128
  10.1 541.2 %reduce-scatter.7.cloned.1.call-start = ((), (), s32[]{:S(2)}) async-start(), calls=%async_computation.9 | async-start | bytes 2433024 | tf_op jit(solution)/shard_map/reduce_scatter | solution.py:154
  10.1 54.8 %copy-start = (bf16[2,600,768]{2,1,0:T(8,128)(2,1)S(1)}, bf16[2,600,768]{2,1,0:T(8,128)(2,1)}, u32[]{:S(2)}) copy-start(bf16[2,600,768]{2,1,0:T(8,128)(2,1)} %param.20) | copy-start | bytes 5529604
  12.1 2.3 copy-start.24
  14.4 52.9 %copy-start.15 = (f32[1200]{0:T(1024)}, f32[1200]{0:T(1024)S(1)}, u32[]{:S(2)}) copy-start(f32[1200]{0:T(1024)S(1)} %div.35) | copy-start | bytes 14404
  14.5 46.5 %copy-start.22 = (f32[2,600]{1,0:T(2,128)}, f32[2,600]{1,0:T(2,128)S(1)}, u32[]{:S(2)}) copy-start(f32[2,600]{1,0:T(2,128)S(1)} %compare_convert_fusion) | copy-start | bytes 14404
  14.6 52.7 %copy-start.17 = (f32[1200]{0:T(1024)}, f32[1200]{0:T(1024)S(1)}, u32[]{:S(2)}) copy-start(f32[1200]{0:T(1024)S(1)} %reshape.369) | copy-start | bytes 14404
  14.6 52.7 %copy-start.28 = (f32[2,600]{1,0:T(2,128)}, f32[2,600]{1,0:T(2,128)S(1)}, u32[]{:S(2)}) copy-start(f32[2,600]{1,0:T(2,128)S(1)} %add_rsqrt_fusion.1) | copy-start | bytes 14404
  59.2 14.7 %copy-start.30 = (f32[768]{0:T(1024)}, f32[768]{0:T(1024)S(1)}, u32[]{:S(2)}) copy-start(f32[768]{0:T(1024)S(1)} %convert_element_type.142) | copy-start | bytes 9220
  59.8 14.1 %copy-start.39 = (f32[768]{0:T(1024)}, f32[768]{0:T(1024)S(1)}, u32[]{:S(2)}) copy-start(f32[768]{0:T(1024)S(1)} %convert_element_type.143) | copy-start | bytes 9220
  61.1 6.1 copy-start.20
  84.0 8.8 %copy-start.12 = (s32[2,600]{1,0:T(2,128)S(1)}, s32[2,600]{1,0:T(2,128)}, u32[]{:S(2)}) copy-start(s32[2,600]{1,0:T(2,128)} %param.22) | copy-start | bytes 14404
  92.8 78.2 %copy-start.1 = (bf16[2,600,768]{2,1,0:T(8,128)(2,1)S(1)}, bf16[2,600,768]{2,1,0:T(8,128)(2,1)}, u32[]{:S(2)}) copy-start(bf16[2,600,768]{2,1,0:T(8,128)(2,1)} %param.20) | copy-start | bytes 5529604
  92.8 78.2 %copy-start.41 = (f32[768]{0:T(1024)S(1)}, f32[768]{0:T(1024)}, u32[]{:S(2)}) copy-start(f32[768]{0:T(1024)} %convert_element_type.147) | copy-start | bytes 9220
  174.7 1.9 copy-start.5
  174.7 20.5 %copy-start.32 = (f32[768]{0:T(1024)S(1)}, f32[768]{0:T(1024)}, u32[]{:S(2)}) copy-start(f32[768]{0:T(1024)} %convert_element_type.148) | copy-start | bytes 9220
  174.7 20.4 %copy-start.35 = (f32[3072]{0:T(1024)S(1)}, f32[3072]{0:T(1024)}, u32[]{:S(2)}) copy-start(f32[3072]{0:T(1024)} %convert_element_type.151) | copy-start | bytes 36868
  174.7 20.4 %copy-start.37 = (f32[768]{0:T(1024)S(1)}, f32[768]{0:T(1024)}, u32[]{:S(2)}) copy-start(f32[768]{0:T(1024)} %convert_element_type.149) | copy-start | bytes 9220
  174.7 114.9 %copy-start.13 = (f32[1200]{0:T(1024)}, f32[1200]{0:T(1024)S(1)}, u32[]{:S(2)}) copy-start(f32[1200]{0:T(1024)S(1)} %broadcast_multiply_fusion.4) | copy-start | bytes 14404
  177.2 112.5 %copy-start.26 = (f32[1200]{0:T(1024)}, f32[1200]{0:T(1024)S(1)}, u32[]{:S(2)}) copy-start(f32[1200]{0:T(1024)S(1)} %add_rsqrt_fusion) | copy-start | bytes 14404
  177.2 83.2 %copy-start.10 = (bf16[1200,768]{1,0:T(8,128)(2,1)S(1)}, bf16[1200,768]{1,0:T(8,128)(2,1)}, u32[]{:S(2)}) copy-start(bf16[1200,768]{1,0:T(8,128)(2,1)} %fusion.27) | copy-start | bytes 5529604
  260.4 18.6 %copy-start.6 = (f32[1200,768]{1,0:T(8,128)S(1)}, f32[1200,768]{1,0:T(8,128)}, u32[]{:S(2)}) copy-start(f32[1200,768]{1,0:T(8,128)} %copy-done.5) | copy-start | bytes 11059204
  260.4 18.6 %copy-start.46 = (bf16[768,3072]{1,0:T(8,128)(2,1)S(1)}, bf16[768,3072]{1,0:T(8,128)(2,1)}, u32[]{:S(2)}) copy-start(bf16[768,3072]{1,0:T(8,128)(2,1)} %all-gather.9.cloned.1.call-done) | copy-start | bytes 14155780
  279.0 10.6 %copy-start.3 = (bf16[2,600,768]{2,1,0:T(8,128)(2,1)S(1)}, bf16[2,600,768]{2,1,0:T(8,128)(2,1)}, u32[]{:S(2)}) copy-start(bf16[2,600,768]{2,1,0:T(8,128)(2,1)} %param.35) | copy-start | bytes 5529604
  279.0 10.6 %copy-start.18 = (f32[1200]{0:T(1024)S(1)}, f32[1200]{0:T(1024)}, u32[]{:S(2)}) copy-start(f32[1200]{0:T(1024)} %copy-done.17) | copy-start | bytes 14404
  289.7 4.2 copy-start.47
  292.0 1.9 copy-start.8
  293.9 3.3 copy-start.48
  297.1 254.1 %reduce-scatter.5.cloned.1.call-start = ((), (), s32[]{:S(2)}) async-start(), calls=%async_computation.8 | async-start | bytes 7299072 | tf_op jit(solution)/shard_map/reduce_scatter | solution.py:152
  302.1 116.0 %copy-start.25 = (f32[2,600]{1,0:T(2,128)S(1)}, f32[2,600]{1,0:T(2,128)}, u32[]{:S(2)}) copy-start(f32[2,600]{1,0:T(2,128)} %copy-done.24) | copy-start | bytes 14404
  302.1 116.0 %copy-start.29 = (f32[2,600]{1,0:T(2,128)S(1)}, f32[2,600]{1,0:T(2,128)}, u32[]{:S(2)}) copy-start(f32[2,600]{1,0:T(2,128)} %copy-done.28) | copy-start | bytes 14404
  302.1 116.1 %copy-start.31 = (f32[768]{0:T(1024)S(1)}, f32[768]{0:T(1024)}, u32[]{:S(2)}) copy-start(f32[768]{0:T(1024)} %copy-done.30) | copy-start | bytes 9220
  302.1 116.1 %copy-start.40 = (f32[768]{0:T(1024)S(1)}, f32[768]{0:T(1024)}, u32[]{:S(2)}) copy-start(f32[768]{0:T(1024)} %copy-done.39) | copy-start | bytes 9220
  429.9 1.5 copy-start.11
  429.9 260.5 %reduce-scatter.11.cloned.1.call-start = ((), (), s32[]{:S(2)}) async-start(), calls=%async_computation.11 | async-start | bytes 9732096 | tf_op jit(solution)/shard_map/reduce_scatter | solution.py:160
  444.9 0.7 copy-start.14
  444.9 0.7 copy-start.27
  444.9 0.7 copy-start.33
  444.9 0.7 copy-start.38
  444.9 387.5 %reduce-scatter.9.cloned.1.call-start = ((), (), s32[]{:S(2)}) async-start(), calls=%async_computation.10 | async-start | bytes 9732096 | tf_op jit(solution)/shard_map/reduce_scatter | solution.py:158
  458.8 1.6 copy-start.4
  458.8 1.6 copy-start.23
  469.8 3.8 copy-start.2
  469.8 4.4 copy-start.9
  469.8 4.4 copy-start.16
  469.8 4.4 copy-start.21
  474.2 10.7 %copy-start.34 = (f32[768]{0:T(1024)S(1)}, f32[768]{0:T(1024)}, u32[]{:S(2)}) copy-start(f32[768]{0:T(1024)} %get-tuple-element.178) | copy-start | bytes 9220
  474.2 10.7 %copy-start.36 = (f32[3072]{0:T(1024)S(1)}, f32[3072]{0:T(1024)}, u32[]{:S(2)}) copy-start(f32[3072]{0:T(1024)} %get-tuple-element.198) | copy-start | bytes 36868
  474.2 10.7 %copy-start.42 = (f32[768]{0:T(1024)S(1)}, f32[768]{0:T(1024)}, u32[]{:S(2)}) copy-start(f32[768]{0:T(1024)} %get-tuple-element.126) | copy-start | bytes 9220
  474.2 10.7 %copy-start.43 = (f32[768]{0:T(1024)S(1)}, f32[768]{0:T(1024)}, u32[]{:S(2)}) copy-start(f32[768]{0:T(1024)} %get-tuple-element.131) | copy-start | bytes 9220
  531.8 5.2 copy-start.7
  531.8 5.2 copy-start.19
  (1 other events, 0.7 us)
Sparse Core Ops, SparseCore 0:
  11.0 62.8 all-gather.4
  76.8 52.8 all-gather.6
  132.6 62.5 all-gather.8
  197.9 62.4 all-gather.10
  297.3 97.8 reduce-scatter.6
  430.0 118.9 reduce-scatter.4
  555.5 134.8 reduce-scatter.10
  697.9 134.5 reduce-scatter.8
where the time goes:
time: 848 us; the launch traced here: 839 us
  waiting for transfers between devices  361 us (43%)
  matrix products  243 us (29%)
  blocking collectives  84.9 us (10%)
  other arithmetic  78.9 us (9%)
  local copies, waits for them, and re-layouts  55.3 us (7%)
  between operations  14.8 us (2%)
    reduce_scatter x1, waiting for transfers between devices, reduce_grads(): lax.psum_scatter(w_up, ('wide', 'narrow'), scatter_dimension=0, tiled=True)  142 us
    reduce_scatter x1, waiting for transfers between devices, reduce_grads(): lax.psum_scatter(w_down, ('wide', 'narrow'), scatter_dimension=0, tiled=T...  139 us
    unnamed x2, blocking collectives  84.9 us
    all_gather x1, waiting for transfers between devices, fetch(): lax.all_gather(w_down, ('wide', 'narrow'), axis=0, tiled=True)  52.9 us
    dot_general x4, matrix products, score_table(): jnp.einsum('qhd,khd->hqk', queries, key_rows, preferred_element_type=jnp....  32.6 us
    convert_element_type x2, other arithmetic, attend_backward(): (probs * (d_probs - jnp.sum(probs * d_probs, axis=-1, keepdims=True))).as...  26.5 us
    dot_general x2, matrix products, attend_backward(): jnp.einsum('qhd,khd->hqk', d_heads, value_rows, preferred_element_type=jn...  26.4 us
    dot_general x2, matrix products, attend_forward(): jnp.einsum('hqk,khd->qhd', probs_low, head_split(qkv_item, 2), preferred_...  26 us
  transfers between devices with their start and end apart: 8, of which 5 were waited for; matrix products, arithmetic and copies ran while one was open for 40% of the time, Pallas kernels for 0%

commit v1 on v0

v1 whole, which is shorter than its diff:
```python
import jax
import jax.numpy as jnp
from jax import lax
from jax.experimental import pallas as pl
from jax.experimental.pallas import tpu as pltpu
from jax.sharding import PartitionSpec as P

D = 768
HEADS = 12
HEAD = 64
GROUP = 256
GROUPS = D // GROUP
PAIRS = GROUP // 128
EPS = 1e-05
MASKED = -1e30
AXES = ("wide", "narrow")
BF = jnp.bfloat16
F32 = jnp.float32
MIB = 1 << 20
VEC_ROWS = 16
SMALL = 128


def mm(a, b):
    return jnp.dot(a, b, preferred_element_type=F32)


def mm_nt(a, b):
    return lax.dot_general(a, b, (((1,), (1,)), ((), ())), preferred_element_type=F32)


def mm_tn(a, b):
    return lax.dot_general(a, b, (((0,), (0,)), ((), ())), preferred_element_type=F32)


def norm_parts(x):
    centred = x - jnp.mean(x, axis=-1, keepdims=True)
    inverse = lax.rsqrt(jnp.mean(centred * centred, axis=-1, keepdims=True) + EPS)
    return centred * inverse, inverse


def norm_back(d_normed, scaled, inverse, gain):
    h = d_normed * gain
    return inverse * (
        h
        - jnp.mean(h, axis=-1, keepdims=True)
        - scaled * jnp.mean(h * scaled, axis=-1, keepdims=True)
    )


def lane_mask(half, value):
    lane = lax.broadcasted_iota(jnp.int32, (1, 128), 1)
    return jnp.where((lane // HEAD) == half, value, 0.0).astype(BF)


def forward_kernel(
    tok_ref, wq_ref, wk_ref, wv_ref, vec_ref, bias_ref, kend_ref,
    n1_ref, q_ref, k_ref, v_ref, mixed_ref, lse_ref,
):
    slots = tok_ref.shape[1]

    @pl.when(pl.program_id(1) == 0)
    def _():
        scaled, _inverse = norm_parts(tok_ref[0].astype(F32))
        n1_ref[0] = (scaled * vec_ref[0:1, :] + vec_ref[1:2, :]).astype(BF)

    n1 = n1_ref[0]
    q_ref[0] = (mm(n1, wq_ref[...]) + bias_ref[2:3, :]).astype(BF)
    k_ref[0] = mm(n1, wk_ref[...]).astype(BF)
    v_ref[0] = (mm(n1, wv_ref[...]) + bias_ref[3:4, :]).astype(BF)
    rows = slots // 3
    lane = lax.broadcasted_iota(jnp.int32, (1, 128), 1)
    lse_parts = []
    for part in range(3):
        at = slice(part * rows, (part + 1) * rows)
        column = lax.broadcasted_iota(jnp.int32, (rows, slots), 1)
        allowed = column < kend_ref[0, at, :]
        lse_lanes = jnp.zeros((rows, 128), F32)
        for pair in range(PAIRS):
            cols = slice(pair * 128, (pair + 1) * 128)
            k2 = k_ref[0, :, cols]
            v2 = v_ref[0, :, cols]
            q2 = q_ref[0, at, cols]
            outs = []
            for half in range(2):
                scores = mm_nt(q2 * lane_mask(half, HEAD ** -0.5), k2)
                scores = jnp.where(allowed, scores, MASKED)
                peak = jnp.max(scores, axis=-1, keepdims=True)
                exponent = jnp.exp(scores - peak)
                total = jnp.sum(exponent, axis=-1, keepdims=True)
                probs = (exponent * (1.0 / total)).astype(BF)
                outs.append(mm(probs, v2))
                lse_lanes = jnp.where(lane == 2 * pair + half, peak + jnp.log(total), lse_lanes)
            mixed_ref[0, at, cols] = jnp.where(lane < HEAD, outs[0], outs[1]).astype(BF)
        lse_parts.append(lse_lanes)
    lse_ref[0] = jnp.concatenate(lse_parts, axis=0).T[:8, :]


def attention_forward(tokens, w_qk, w_v, vec, kend):
    items, slots, _ = tokens.shape
    rows = lambda i, g: (i, 0, 0)
    cols = lambda i, g: (i, 0, g)
    return pl.pallas_call(
        forward_kernel,
        grid=(items, GROUPS),
        in_specs=[
            pl.BlockSpec((1, slots, D), rows),
            pl.BlockSpec((D, GROUP), lambda i, g: (0, g)),
            pl.BlockSpec((D, GROUP), lambda i, g: (0, GROUPS + g)),
            pl.BlockSpec((D, GROUP), lambda i, g: (0, g)),
            pl.BlockSpec((VEC_ROWS, D), lambda i, g: (0, 0)),
            pl.BlockSpec((VEC_ROWS, GROUP), lambda i, g: (0, g)),
            pl.BlockSpec((1, slots, 1), rows),
        ],
        out_specs=[
            pl.BlockSpec((1, slots, D), rows),
            pl.BlockSpec((1, slots, GROUP), cols),
            pl.BlockSpec((1, slots, GROUP), cols),
            pl.BlockSpec((1, slots, GROUP), cols),
            pl.BlockSpec((1, slots, GROUP), cols),
            pl.BlockSpec((1, 8, slots), lambda i, g: (i, g, 0)),
        ],
        out_shape=[jax.ShapeDtypeStruct((items, slots, D), BF)] * 5
        + [jax.ShapeDtypeStruct((items, 8 * GROUPS, slots), F32)],
        compiler_params=pltpu.CompilerParams(vmem_limit_bytes=48 * MIB),
        cost_estimate=pl.CostEstimate(
            flops=2 * items * slots * D * 3 * D + 16 * items * HEADS * slots * slots * HEAD,
            bytes_accessed=30 * MIB,
            transcendentals=items * HEADS * slots * slots,
        ),
        name="attention_forward",
    )(tokens, w_qk, w_qk, w_v, vec, vec, kend)


GELU_SCALE = 0.7978845608028654
GELU_CUBE = 0.044715


def row_valid(len_ref, start, rows, slots, items):
    index = lax.broadcasted_iota(jnp.int32, (rows, 1), 0) + start
    valid = index < len_ref[0]
    for item in range(1, items):
        valid = valid | ((index >= item * slots) & (index < item * slots + len_ref[item]))
    return jnp.where(valid, 1.0, 0.0).astype(F32)


def mlp_kernel(stacked, items, slots):
    row_count = items * slots
    tile = row_count // 3

    def kernel(
        len_ref, mixed_ref, tok_ref, cot_ref, wout_ref, vec_ref, up_ref, down_ref,
        middle_ref, out_ref, dn2_ref, gbd_ref, gbu_ref, *rest,
    ):
        if stacked:
            grads = rest[0]
            n2, dlow, act, dpre, oacc, gu, gd, sems = rest[1:]
        else:
            gu_out, gd_out = rest[:2]
            n2, dlow, act, dpre, oacc, gu, gd, sems = rest[2:]
        b = pl.program_id(0)
        last = pl.num_programs(0) - 1
        slot = lax.rem(b, 2)

        def copies(step, where):
            if stacked:
                per = gu.shape[2]
                up_to = grads.at[:, pl.ds(pl.multiple_of(per * step, 8), per), :]
                down_to = grads.at[
                    pl.ds(gd.shape[1] * step, gd.shape[1]), 4 * per : 8 * per, :
                ]
            else:
                up_to = gu_out.at[:, pl.ds(pl.multiple_of(D * step, D), D)]
                down_to = gd_out.at[pl.ds(pl.multiple_of(D * step, D), D), :]
            return (
                pltpu.make_async_copy(gu.at[where], up_to, sems.at[0, where]),
                pltpu.make_async_copy(gd.at[where], down_to, sems.at[1, where]),
            )

        @pl.when(b == 0)
        def _():
            sums = jnp.zeros((1, D), F32)
            for part in range(3):
                at = slice(part * tile, (part + 1) * tile)
                middle = (
                    tok_ref[at, :].astype(F32) + mm(mixed_ref[at, :], wout_ref[...])
                ) + vec_ref[4:5, :]
                middle_ref[at, :] = middle
                scaled, _inverse = norm_parts(middle)
                n2[at, :] = (scaled * vec_ref[5:6, :] + vec_ref[6:7, :]).astype(BF)
                valid = row_valid(len_ref, part * tile, tile, slots, items)
                lower = cot_ref[at, :].astype(F32) * valid
                dlow[at, :] = lower.astype(BF)
                sums = sums + jnp.sum(lower, axis=0, keepdims=True)
            gbd_ref[...] = jnp.broadcast_to(sums, gbd_ref.shape)

        up = up_ref[...].reshape(D, D)
        down = down_ref[...].reshape(D, D)
        bias = vec_ref[pl.ds(8 + b, 1), :]
        sums = jnp.zeros((1, D), F32)
        for part in range(3):
            at = slice(part * tile, (part + 1) * tile)
            pre = mm(n2[at, :], up) + bias
            square = pre * pre
            half_t = 0.5 * jnp.tanh(GELU_SCALE * pre * (1.0 + GELU_CUBE * square))
            cdf = 0.5 + half_t
            active = (pre * cdf).astype(BF)
            act[at, :] = active
            slope = cdf + pre * (0.5 - 2.0 * half_t * half_t) * (
                GELU_SCALE + (3.0 * GELU_CUBE * GELU_SCALE) * square
            )
            d_pre = (mm_nt(dlow[at, :], down) * slope).astype(BF)
            dpre[at, :] = d_pre
            sums = sums + jnp.sum(d_pre.astype(F32), axis=0, keepdims=True)
            branch = mm(active, down)
            d_n2 = mm_nt(d_pre, up)

            @pl.when(b == 0)
            def _():
                oacc[at, :] = branch
                dn2_ref[at, :] = d_n2

            @pl.when(b > 0)
            def _():
                oacc[at, :] += branch
                dn2_ref[at, :] += d_n2

        gbu_ref[...] = jnp.broadcast_to(sums, gbu_ref.shape)

        @pl.when(b >= 2)
        def _():
            for copy in copies(b - 2, slot):
                copy.wait()

        gu[slot] = mm_tn(n2[...], dpre[...]).reshape(gu.shape[1:]).astype(BF)
        gd[slot] = mm_tn(act[...], dlow[...]).reshape(gd.shape[1:]).astype(BF)
        for copy in copies(b, slot):
            copy.start()

        @pl.when(b == last)
        def _():
            for part in range(3):
                at = slice(part * tile, (part + 1) * tile)
                valid = row_valid(len_ref, part * tile, tile, slots, items)
                whole = middle_ref[at, :] + (oacc[at, :] + vec_ref[7:8, :])
                out_ref[at, :] = (whole * valid).astype(BF)
            for step, where in ((last - 1, 1 - slot), (last, slot)):
                for copy in copies(step, where):
                    copy.wait()

    return kernel


def feed_forward(lengths, mixed, tokens, cotangent, w_vo, vec, up, down, stacked, items, slots):
    row_count = items * slots
    steps = 4
    once = pl.Buffered(1)
    fixed = lambda b, *_: (0, 0)
    if stacked:
        devices, stack, _ = up.shape
        per = stack // 8
        up_spec = pl.BlockSpec((devices, per, D), lambda b, *_: (0, b, 0))
        down_spec = pl.BlockSpec((devices // 4, 4 * per, D), lambda b, *_: (b, 1, 0))
        grad_shapes = [jax.ShapeDtypeStruct((devices, stack, D), BF)]
        gu_shape, gd_shape = (devices, per, D), (devices // 4, 4 * per, D)
    else:
        up_spec = pl.BlockSpec((D, D), lambda b, *_: (0, b))
        down_spec = pl.BlockSpec((D, D), lambda b, *_: (b, 0))
        grad_shapes = [
            jax.ShapeDtypeStruct((D, steps * D), BF),
            jax.ShapeDtypeStruct((steps * D, D), BF),
        ]
        gu_shape = gd_shape = (D, D)
    return pl.pallas_call(
        mlp_kernel(stacked, items, slots),
        grid_spec=pltpu.PrefetchScalarGridSpec(
            num_scalar_prefetch=1,
            grid=(steps,),
            in_specs=[
                pl.BlockSpec((row_count, D), fixed, pipeline_mode=once),
                pl.BlockSpec((row_count, D), fixed, pipeline_mode=once),
                pl.BlockSpec((row_count, D), fixed, pipeline_mode=once),
                pl.BlockSpec((D, D), lambda b, *_: (0, 1), pipeline_mode=once),
                pl.BlockSpec((VEC_ROWS, D), fixed),
                up_spec,
                down_spec,
            ],
            out_specs=[
                pl.BlockSpec((row_count, D), fixed, pipeline_mode=once),
                pl.BlockSpec((row_count, D), fixed, pipeline_mode=once),
                pl.BlockSpec((row_count, D), fixed, pipeline_mode=once),
                pl.BlockSpec((8, D), fixed),
                pl.BlockSpec((8, D), lambda b, *_: (0, b)),
            ]
            + [pl.BlockSpec(memory_space=pl.ANY)] * len(grad_shapes),
            scratch_shapes=[
                pltpu.VMEM((row_count, D), BF),
                pltpu.VMEM((row_count, D), BF),
                pltpu.VMEM((row_count, D), BF),
                pltpu.VMEM((row_count, D), BF),
                pltpu.VMEM((row_count, D), F32),
                pltpu.VMEM((2,) + gu_shape, BF),
                pltpu.VMEM((2,) + gd_shape, BF),
                pltpu.SemaphoreType.DMA((2, 2)),
            ],
        ),
        out_shape=[
            jax.ShapeDtypeStruct((row_count, D), F32),
            jax.ShapeDtypeStruct((row_count, D), BF),
            jax.ShapeDtypeStruct((row_count, D), F32),
            jax.ShapeDtypeStruct((8, D), F32),
            jax.ShapeDtypeStruct((8, steps * D), F32),
        ]
        + grad_shapes,
        compiler_params=pltpu.CompilerParams(vmem_limit_bytes=60 * MIB),
        cost_estimate=pl.CostEstimate(
            flops=2 * row_count * D * D * 25,
            bytes_accessed=36 * MIB,
            transcendentals=row_count * 4 * D,
        ),
        name="feed_forward",
    )(lengths, mixed, tokens, cotangent, w_vo, vec, up, down)


def middle_kernel(slots):
    def kernel(
        len_ref, dn2_ref, middle_ref, cot_ref, mixed_ref, wout_ref, vec_ref,
        dmid_ref, dmix_ref, delta_ref, gout_ref, sums_ref, acc,
    ):
        i = pl.program_id(0)
        last = pl.num_programs(0) - 1
        scaled, inverse = norm_parts(middle_ref[0])
        d_n2 = dn2_ref[0]
        valid = jnp.where(
            lax.broadcasted_iota(jnp.int32, (slots, 1), 0) < len_ref[i], 1.0, 0.0
        ).astype(F32)
        d_middle = cot_ref[0].astype(F32) * valid + norm_back(
            d_n2, scaled, inverse, vec_ref[5:6, :]
        )
        dmid_ref[0] = d_middle
        branch = d_middle.astype(BF)
        mixed = mixed_ref[0]
        d_mixed = mm_nt(branch, wout_ref[...]).astype(BF)
        dmix_ref[0] = d_mixed
        product = d_mixed.astype(F32) * mixed.astype(F32)
        row = lax.broadcasted_iota(jnp.int32, (8 * GROUPS, D), 0)
        lane = lax.broadcasted_iota(jnp.int32, (8 * GROUPS, D), 1)
        pick = jnp.where(
            (lane // HEAD == 4 * (row // 8) + row % 8) & (row % 8 < 4), 1.0, 0.0
        ).astype(BF)
        high = product.astype(BF)
        low = (product - high.astype(F32)).astype(BF)
        delta_ref[0] = mm_nt(pick, high) + mm_nt(pick, low)
        sums = jnp.concatenate(
            [
                jnp.sum(d_n2 * scaled, axis=0, keepdims=True),
                jnp.sum(d_n2, axis=0, keepdims=True),
                jnp.sum(branch.astype(F32), axis=0, keepdims=True),
                jnp.zeros((5, D), F32),
            ],
            axis=0,
        )
        part = mm_tn(mixed, branch)

        @pl.when(i == 0)
        def _():
            sums_ref[...] = sums
            acc[...] = part

        @pl.when(i > 0)
        def _():
            sums_ref[...] += sums
            acc[...] += part

        @pl.when(i == last)
        def _():
            gout_ref[...] = acc[...].astype(BF)

    return kernel


def middle_backward(lengths, d_n2, middle, cotangent, mixed, w_vo, vec):
    items, slots, _ = mixed.shape
    rows = lambda i, *_: (i, 0, 0)
    fixed = lambda i, *_: (0, 0)
    block = pl.BlockSpec((1, slots, D), rows)
    return pl.pallas_call(
        middle_kernel(slots),
        grid_spec=pltpu.PrefetchScalarGridSpec(
            num_scalar_prefetch=1,
            grid=(items,),
            in_specs=[
                block, block, block, block,
                pl.BlockSpec((D, D), lambda i, *_: (0, 1)),
                pl.BlockSpec((VEC_ROWS, D), fixed),
            ],
            out_specs=[
                block, block,
                pl.BlockSpec((1, 8 * GROUPS, slots), rows),
                pl.BlockSpec((D, D), fixed),
                pl.BlockSpec((8, D), fixed),
            ],
            scratch_shapes=[pltpu.VMEM((D, D), F32)],
        ),
        out_shape=[
            jax.ShapeDtypeStruct((items, slots, D), F32),
            jax.ShapeDtypeStruct((items, slots, D), BF),
            jax.ShapeDtypeStruct((items, 8 * GROUPS, slots), F32),
            jax.ShapeDtypeStruct((D, D), BF),
            jax.ShapeDtypeStruct((8, D), F32),
        ],
        compiler_params=pltpu.CompilerParams(vmem_limit_bytes=56 * MIB),
        cost_estimate=pl.CostEstimate(
            flops=4 * items * slots * D * D, bytes_accessed=18 * MIB, transcendentals=0
        ),
        name="middle_backward",
    )(lengths, d_n2, middle, cotangent, mixed, w_vo, vec)


def backward_kernel(
    q_ref, k_ref, v_ref, dmix_ref, lse_ref, delta_ref, kend_ref, n1_ref,
    wq_ref, wk_ref, wv_ref, tok_ref, dmid_ref, vec_ref,
    gq_ref, gk_ref, gv_ref, grad_ref, gbias_ref, sums_ref,
    dqkv, dn1, acc,
):
    g = pl.program_id(0)
    i = pl.program_id(1)
    last_group = pl.num_programs(0) - 1
    last_item = pl.num_programs(1) - 1
    slots = q_ref.shape[1]
    key = lax.broadcasted_iota(jnp.int32, (slots, slots), 0)
    allowed = key < kend_ref[0]
    for pair in range(PAIRS):
        cols = slice(pair * 128, (pair + 1) * 128)
        q2 = q_ref[0, :, cols]
        k2 = k_ref[0, :, cols]
        v2 = v_ref[0, :, cols]
        o2 = dmix_ref[0, :, cols]
        dq = dk = dv = None
        for half in range(2):
            head = 2 * pair + half
            qm = q2 * lane_mask(half, HEAD ** -0.5)
            km = k2 * lane_mask(half, 1.0)
            om = o2 * lane_mask(half, 1.0)
            scores = mm_nt(k2, qm)
            probs = jnp.exp(
                jnp.where(allowed, scores, MASKED) - lse_ref[0, head : head + 1, :]
            )
            d_probs = mm_nt(v2, om)
            d_scores = (probs * (d_probs - delta_ref[0, head : head + 1, :])).astype(BF)
            dv_half = mm(probs.astype(BF), om)
            dk_half = mm(d_scores, qm)
            dq_half = mm_tn(d_scores, km)
            dv = dv_half if dv is None else dv + dv_half
            dk = dk_half if dk is None else dk + dk_half
            dq = dq_half if dq is None else dq + dq_half
        dqkv[:, pair * 128 : (pair + 1) * 128] = (dq * HEAD ** -0.5).astype(BF)
        dqkv[:, GROUP + pair * 128 : GROUP + (pair + 1) * 128] = dk.astype(BF)
        dqkv[:, 2 * GROUP + pair * 128 : 2 * GROUP + (pair + 1) * 128] = dv.astype(BF)
    packed = dqkv[...]
    bias = jnp.sum(packed.astype(F32), axis=0, keepdims=True)
    bias = jnp.broadcast_to(bias, gbias_ref.shape)
    part = mm_tn(n1_ref[0], packed)

    @pl.when(i == 0)
    def _():
        acc[...] = part
        gbias_ref[...] = bias

    @pl.when(i > 0)
    def _():
        acc[...] += part
        gbias_ref[...] += bias

    @pl.when(i == last_item)
    def _():
        gq_ref[...] = acc[:, :GROUP].astype(BF)
        gk_ref[...] = acc[:, GROUP : 2 * GROUP].astype(BF)
        gv_ref[...] = acc[:, 2 * GROUP :].astype(BF)

    d_n1 = (
        mm_nt(packed[:, :GROUP], wq_ref[...])
        + mm_nt(packed[:, GROUP : 2 * GROUP], wk_ref[...])
        + mm_nt(packed[:, 2 * GROUP :], wv_ref[...])
    )

    @pl.when(g == 0)
    def _():
        dn1[i] = d_n1

    @pl.when(g > 0)
    def _():
        dn1[i] += d_n1

    @pl.when(g == last_group)
    def _():
        scaled, inverse = norm_parts(tok_ref[0].astype(F32))
        whole = dn1[i]
        grad_ref[0] = dmid_ref[0] + norm_back(whole, scaled, inverse, vec_ref[0:1, :])
        sums = jnp.concatenate(
            [
                jnp.sum(whole * scaled, axis=0, keepdims=True),
                jnp.sum(whole, axis=0, keepdims=True),
                jnp.zeros((6, D), F32),
            ],
            axis=0,
        )

        @pl.when(i == 0)
        def _():
            sums_ref[...] = sums

        @pl.when(i > 0)
        def _():
            sums_ref[...] += sums


def attention_backward(q, k, v, d_mixed, lse, delta, kend_row, n1, w_qk, w_v, tokens, d_middle, vec):
    items, slots, _ = q.shape
    rows = lambda g, i: (i, 0, 0)
    cols = lambda g, i: (i, 0, g)
    late = lambda g, i: (jnp.where(g == GROUPS - 1, i, 0), 0, 0)
    block = pl.BlockSpec((1, slots, GROUP), cols)
    table = pl.BlockSpec((1, 8, slots), lambda g, i: (i, g, 0))
    weight = pl.BlockSpec((D, GROUP), lambda g, i: (0, g))
    return pl.pallas_call(
        backward_kernel,
        grid=(GROUPS, items),
        in_specs=[
            block, block, block, block, table, table,
            pl.BlockSpec((1, 1, slots), rows),
            pl.BlockSpec((1, slots, D), rows),
            weight,
            pl.BlockSpec((D, GROUP), lambda g, i: (0, GROUPS + g)),
            weight,
            pl.BlockSpec((1, slots, D), late),
            pl.BlockSpec((1, slots, D), late),
            pl.BlockSpec((VEC_ROWS, D), lambda g, i: (0, 0)),
        ],
        out_specs=[
            weight, weight, weight,
            pl.BlockSpec((1, slots, D), late),
            pl.BlockSpec((8, 3 * GROUP), lambda g, i: (0, g)),
            pl.BlockSpec((8, D), lambda g, i: (0, 0)),
        ],
        out_shape=[jax.ShapeDtypeStruct((D, D), BF)] * 3
        + [
            jax.ShapeDtypeStruct((items, slots, D), F32),
            jax.ShapeDtypeStruct((8, 3 * D), F32),
            jax.ShapeDtypeStruct((8, D), F32),
        ],
        scratch_shapes=[
            pltpu.VMEM((slots, 3 * GROUP), BF),
            pltpu.VMEM((items, slots, D), F32),
            pltpu.VMEM((D, 3 * GROUP), F32),
        ],
        compiler_params=pltpu.CompilerParams(vmem_limit_bytes=56 * MIB),
        cost_estimate=pl.CostEstimate(
            flops=4 * items * slots * D * 3 * D + 40 * items * HEADS * slots * slots * HEAD,
            bytes_accessed=36 * MIB,
            transcendentals=items * HEADS * slots * slots,
        ),
        name="attention_backward",
    )(q, k, v, d_mixed, lse, delta, kend_row, n1, w_qk, w_qk, w_v, tokens, d_middle, vec)


def swap(x, axis, bit, size):
    return lax.ppermute(x, axis, [(i, i ^ (1 << bit)) for i in range(size)])


def own_bit(axis, bit):
    return (lax.axis_index(axis) >> bit) & 1


def doubled(x, axis, bit, size, at):
    other = jnp.expand_dims(swap(x, axis, bit, size), at)
    mine = jnp.expand_dims(x, at)
    return jnp.where(
        own_bit(axis, bit) == 0,
        jnp.concatenate([mine, other], at),
        jnp.concatenate([other, mine], at),
    )


def halved(x, axis, bit, size, at):
    me = own_bit(axis, bit)
    send = lax.dynamic_index_in_dim(x, 1 - me, at, keepdims=False).astype(BF)
    keep = lax.dynamic_index_in_dim(x, me, at, keepdims=False)
    return keep.astype(F32) + swap(send, axis, bit, size).astype(F32)


def gather_rows(x, cut, sizes):
    rows = x.shape[0]
    wide, narrow = sizes
    if sizes != (8, 4):
        whole = lax.all_gather(x, AXES, axis=0, tiled=True)
        return whole[:, :cut], whole[:, cut:]
    x = doubled(x, "wide", 2, wide, 0)
    x = doubled(x, "wide", 1, wide, 1)
    a, b = x[..., :cut], x[..., cut:]
    a = doubled(a, "wide", 0, wide, 2)
    b = doubled(b, "narrow", 1, narrow, 2)
    a = doubled(a, "narrow", 1, narrow, 3)
    b = doubled(b, "wide", 0, wide, 2)
    a = doubled(a, "narrow", 0, narrow, 4)
    b = doubled(b, "narrow", 0, narrow, 4)
    count = wide * narrow * rows
    return a.reshape(count, -1), b.reshape(count, -1)


def scatter_rows(a, b, sizes):
    wide, narrow = sizes
    if sizes != (8, 4):
        scatter = lambda x: lax.psum_scatter(
            x.astype(F32), AXES, scatter_dimension=0, tiled=True
        )
        return scatter(a), scatter(b)
    rows = a.shape[0] // (wide * narrow)
    split = (2, 2, 2, 2, 2, rows, -1)
    a = halved(a.reshape(split), "narrow", 0, narrow, 4)
    b = halved(b.reshape(split), "narrow", 0, narrow, 4)
    a = halved(a, "narrow", 1, narrow, 3)
    b = halved(b, "wide", 0, wide, 2)
    a = halved(a, "wide", 0, wide, 2)
    b = halved(b, "narrow", 1, narrow, 2)
    cut = a.shape[-1]
    x = jnp.concatenate([a, b], axis=-1)
    x = halved(x, "wide", 1, wide, 1)
    x = halved(x, "wide", 2, wide, 0)
    return x[:, :cut], x[:, cut:]


def body(sizes):
    def run(
        tokens, lengths, blocks, ln1_gain, ln1_bias, qkv_weight, qv_bias, out_weight, out_bias,
        ln2_gain, ln2_bias, up_weight, up_bias, down_weight, down_bias, cotangent,
    ):
        items, slots, _ = tokens.shape
        row_count = items * slots
        rows = qkv_weight.shape[0]
        devices = sizes[0] * sizes[1]
        stacked = rows % 8 == 0

        if stacked:
            pack = jnp.concatenate(
                [up_weight[:, b * D : (b + 1) * D] for b in range(4)] + [down_weight], axis=0
            )
            whole_ffn = lax.all_gather(pack, AXES, axis=0, tiled=True)
            up = down = whole_ffn.reshape(devices, 8 * rows, D)
        else:
            up = lax.all_gather(up_weight, AXES, axis=0, tiled=True)
            down = lax.all_gather(down_weight, AXES, axis=0, tiled=True)

        column = lambda v: v.reshape(rows, -1)
        small = jnp.concatenate(
            [
                column(ln1_gain), column(ln1_bias), column(qv_bias), column(out_bias),
                column(ln2_gain), column(ln2_bias), column(up_bias), column(down_bias),
            ],
            axis=1,
        )
        small = jnp.pad(small, ((0, 0), (0, SMALL - small.shape[1])))
        first = jnp.concatenate([qkv_weight, out_weight, small], axis=1)
        w_qk, w_vo = gather_rows(first, 2 * D, sizes)
        table = w_vo[:, 2 * D :].astype(F32)
        vec = jnp.concatenate(
            [
                table[:, 0:2].T,
                table[:, 2:4].reshape(2, D),
                table[:, 4:7].T,
                table[:, 11:12].T,
                table[:, 7:11].reshape(4, D),
                jnp.zeros((4, D), F32),
            ],
            axis=0,
        )

        ends = jnp.sum(
            (blocks[:, None, :] <= blocks[:, :, None]).astype(jnp.int32), axis=-1
        )
        kend = jnp.minimum(ends, lengths[:, None])

        n1, q, k, v, mixed, lse = attention_forward(
            tokens, w_qk, w_vo, vec, kend.reshape(items, slots, 1)
        )
        flat = lambda t: t.reshape(row_count, D)
        cube = lambda t: t.reshape(items, slots, D)
        middle, output, d_n2, gb_down, gb_up, *grads = feed_forward(
            lengths, flat(mixed), flat(tokens), flat(cotangent), w_vo, vec, up, down,
            stacked, items, slots,
        )
        if stacked:
            own = lax.psum_scatter(
                grads[0].reshape(devices * 8 * rows, D), AXES, scatter_dimension=0, tiled=True
            ).astype(F32)
            grad_up = jnp.concatenate(
                [own[b * rows : (b + 1) * rows] for b in range(4)], axis=1
            )
            grad_down = own[4 * rows :]
        else:
            grad_up = lax.psum_scatter(
                grads[0].astype(F32), AXES, scatter_dimension=0, tiled=True
            )
            grad_down = lax.psum_scatter(
                grads[1].astype(F32), AXES, scatter_dimension=0, tiled=True
            )
        d_middle, d_mixed, delta, g_out, sums2 = middle_backward(
            lengths, cube(d_n2), cube(middle), cotangent, mixed, w_vo, vec
        )
        gq, gk, gv, input_grad, gbias, sums1 = attention_backward(
            q, k, v, d_mixed, lse, delta, kend.reshape(items, 1, slots), n1,
            w_qk, w_vo, tokens, d_middle, vec,
        )
        gbias = gbias[0].reshape(GROUPS, 3, GROUP)
        tall = lambda value: value.reshape(D, -1)
        small_grads = jnp.concatenate(
            [
                sums1[0:2].T,
                tall(jnp.concatenate([gbias[:, 0].reshape(D), gbias[:, 2].reshape(D)])),
                sums2[2:3].T,
                sums2[0:2].T,
                tall(gb_up[0]),
                gb_down[0:1].T,
            ],
            axis=1,
        )
        small_grads = jnp.pad(small_grads, ((0, 0), (0, SMALL - small_grads.shape[1])))
        own_qk, own_vo = scatter_rows(
            jnp.concatenate([gq, gk], axis=1),
            jnp.concatenate([gv, g_out, small_grads.astype(BF)], axis=1),
            sizes,
        )
        own_small = own_vo[:, 2 * D :]
        return (
            cube(output),
            input_grad,
            own_small[:, 0],
            own_small[:, 1],
            jnp.concatenate([own_qk, own_vo[:, :D]], axis=1),
            own_small[:, 2:4].reshape(-1),
            own_vo[:, D : 2 * D],
            own_small[:, 4],
            own_small[:, 5],
            own_small[:, 6],
            grad_up,
            own_small[:, 7:11].reshape(-1),
            grad_down,
            own_small[:, 11],
        )

    return run


def solution(mesh):
    sizes = (mesh.shape["wide"], mesh.shape["narrow"])
    one = P(AXES)
    two = P(AXES, None)
    three = P(AXES, None, None)
    return jax.shard_map(
        body(sizes),
        mesh=mesh,
        in_specs=(
            three, one, two, one, one, two, one, two, one, one, one, two, one, two, one, three,
        ),
        out_specs=(
            three, three, one, one, two, one, two, one, one, one, two, one, two, one,
        ),
        check_vma=False,
    )
```

time: 848 us -> 379 us (0.45)
  waiting for transfers between devices: 361 us -> 90.2 us
  matrix products: 243 us -> 0 us
  Pallas kernels: 0 us -> 186 us
  blocking collectives: 84.9 us -> 0 us
  other arithmetic: 78.9 us -> 15.2 us
  starting transfers between devices: 0.31 us -> 21.2 us
  local copies, waits for them, and re-layouts: 55.3 us -> 46.4 us
    reduce_scatter x4 -> x1, waiting for transfers between devices: 281 us -> 0.01 us  [run(): lax.psum_scatter(grads[0].reshape(devices * 8 * rows, D), AXES, scatter_d...]
    dot_general x26 -> x0, matrix products: 243 us -> none  [the longest x4 32.6 us: score_table(): jnp.einsum('qhd,khd->hqk', queries, key_rows, preferred_element_type=jnp....]
    pallas_call x0 -> x4, Pallas kernels: none -> 186 us  [the longest x1 65.1 us: feed_forward(): pl.pallas_call(mlp_kernel(stacked, items, slots), grid_spec=pltpu.Prefetc...]
    ppermute x0 -> x16, waiting for transfers between devices: none -> 90.2 us  [swap(): return lax.ppermute(x, axis, [(i, i ^ 1 << bit) for i in range(size)])]
    unnamed x2 -> x0, blocking collectives: 84.9 us -> none
    all_gather x4 -> x1, waiting for transfers between devices: 77.5 us -> 0.01 us  [run(): whole_ffn = lax.all_gather(pack, AXES, axis=0, tiled=True)]
    convert_element_type x11 -> x2, other arithmetic: 32.1 us -> 0.82 us  [the longest x1 0.77 us: run(): table = w_vo[:, 2 * D:].astype(F32)]
    reduce_sum x8 -> x1, other arithmetic: 31.5 us -> 0.56 us  [run(): jnp.sum((blocks[:, None, :] <= blocks[:, :, None]).astype(jnp.int32), axi...]
  transfers between devices with their start and end apart: 8 -> 18, of which waited for: 5 -> 14; matrix products, arithmetic and copies ran while one was open for 40% -> 14% of each run, Pallas kernels for 0% -> 32%
where the time goes in v1:
time: 379 us; the launch traced here: 374 us
  Pallas kernels  186 us (49%)
  waiting for transfers between devices  90.2 us (24%)
  local copies, waits for them, and re-layouts  46.4 us (12%)
  starting transfers between devices  21.2 us (6%)
  other arithmetic  15.2 us (4%)
  between operations  14.7 us (4%)
    ppermute x16, waiting for transfers between devices, swap(): return lax.ppermute(x, axis, [(i, i ^ 1 << bit) for i in range(size)])  90.2 us
    pallas_call x1, Pallas kernels, feed_forward(): pl.pallas_call(mlp_kernel(stacked, items, slots), grid_spec=pltpu.Prefetc...  65.1 us
    pallas_call x1, Pallas kernels, attention_backward(): pl.pallas_call(backward_kernel, grid=(GROUPS, items), in_specs=[block, bl...  61.3 us
    pallas_call x1, Pallas kernels, attention_forward(): pl.pallas_call(forward_kernel, grid=(items, GROUPS), in_specs=[pl.BlockSp...  45.8 us
    ppermute x16, starting transfers between devices, swap(): return lax.ppermute(x, axis, [(i, i ^ 1 << bit) for i in range(size)])  21.1 us
    pallas_call x1, Pallas kernels, middle_backward(): pl.pallas_call(middle_kernel(slots), grid_spec=pltpu.PrefetchScalarGridSp...  14.2 us
    unnamed x32, local copies, waits for them, and re-layouts  9.85 us
  transfers between devices with their start and end apart: 18, of which 14 were waited for; matrix products, arithmetic and copies ran while one was open for 14% of the time, Pallas kernels for 32%

profile of v1, /device:TPU:0, one launch (start us, length us, event | category | flops | bytes accessed | tf_op | source)
XLA Modules:
  0.0 374.0 jit_solution(9061732030630079889)
XLA Ops:
  7.2 0.8 slice_dynamic-update-slice_fusion.3
  8.0 0.8 slice_dynamic-update-slice_fusion.2
  8.8 0.8 slice_dynamic-update-slice_fusion.1
  9.6 0.8 slice_dynamic-update-slice_fusion
  10.3 0.9 constant_dynamic-update-slice_fusion
  16.5 0.8 reshape.590
  18.2 1.0 fusion.19
  19.1 4.1 %collective-permute-start = (bf16[24,3200]{1,0:T(8,128)(2,1)S(1)}, bf16[24,3200]{1,0:T(8,128)(2,1)S(1)}, u32[]{:S(2)}, u32[]{:S(2)}) collective-permute-start(bf16[24,3200]{1,0:T(8,128)(2,1)S(1)} %get-tuple-element.86), channel_id=1, source_target_pairs={{0,16},{4,20},{8,24},{12,28},{16,0},{20,4},{24,8},{28,12},{1,17},{... | collective-permute-start | bytes 460808 | tf_op jit(solution)/shard_map/ppermute | solution.py:568
  24.9 9.4 %collective-permute-done = bf16[24,3200]{1,0:T(8,128)(2,1)S(1)} collective-permute-done((bf16[24,3200]{1,0:T(8,128)(2,1)S(1)}, bf16[24,3200]{1,0:T(8,128)(2,1)S(1)}, u32[]{:S(2)}, u32[]{:S(2)}) %collective-permute-start) | collective-permute-done | bytes 153632 | tf_op jit(solution)/shard_map/ppermute | solution.py:568
  34.4 2.1 collective-permute-start.1
  36.6 8.2 %collective-permute-done.1 = bf16[2,24,3200]{2,1,0:T(8,128)(2,1)S(1)} collective-permute-done((bf16[2,24,3200]{2,1,0:T(8,128)(2,1)S(1)}, bf16[2,24,3200]{2,1,0:T(8,128)(2,1)S(1)}, u32[]{:S(2)}, u32[]{:S(2)}) %collective-permute-start.1) | collective-permute-done | bytes 307232 | tf_op jit(solution)/shard_map/ppermute | solution.py:568
  45.0 1.6 collective-permute-start.2
  46.7 1.4 collective-permute-start.5
  48.1 9.1 %collective-permute-done.2 = bf16[2,2,24,1536]{3,2,1,0:T(8,128)(2,1)S(1)} collective-permute-done((bf16[2,2,24,1536]{3,2,1,0:T(8,128)(2,1)S(1)}, bf16[2,2,24,1536]{3,2,1,0:T(8,128)(2,1)S(1)}, u32[]{:S(2)}, u32[]{:S(2)}) %collective-permute-start.2) | collective-permute-done | bytes 294944 | tf_op jit(solution)/shard_map/ppermute | solution.py:568
  57.3 1.5 collective-permute-start.3
  59.1 3.5 collective-permute-done.5
  62.7 1.6 collective-permute-start.6
  64.5 10.1 %collective-permute-done.3 = bf16[2,2,2,24,1536]{4,3,1,0,2:T(8,128)(2,1)S(1)} collective-permute-done((bf16[2,2,2,24,1536]{4,3,1,0,2:T(8,128)(2,1)S(1)}, bf16[2,2,2,24,1536]{4,3,1,0,2:T(8,128)(2,1)S(1)}, u32[]{:S(2)}, u32[]{:S(2)}) %collective-permute-start.3) | collective-permute-done | bytes 589856 | tf_op jit(solution)/shard_map/ppermute | solution.py:568
  74.9 6.8 %collective-permute-done.6 = bf16[2,2,2,24,1664]{4,3,2,1,0:T(8,128)(2,1)S(1)} collective-permute-done((bf16[2,2,2,24,1664]{4,3,2,1,0:T(8,128)(2,1)S(1)}, bf16[2,2,2,24,1664]{4,3,2,1,0:T(8,128)(2,1)S(1)}, u32[]{:S(2)}, u32[]{:S(2)}) %collective-permute-start.6) | collective-permute-done | bytes 639008 | tf_op jit(solution)/shard_map/ppermute | solution.py:568
  83.0 1.8 copy.187
  85.7 0.8 slice.161
  86.4 1.2 copy.207
  87.7 0.8 convert_element_type.86
  88.5 0.9 copy.194
  89.4 1.2 reshape.597
  90.6 0.9 copy.193
  91.6 1.3 reshape.596
  95.1 45.8 %attention_forward.1 = (bf16[2,600,768]{2,1,0:T(8,128)(2,1)S(1)}, bf16[2,600,768]{2,1,0:T(8,128)(2,1)S(1)}, bf16[2,600,768]{2,1,0:T(8,128)(2,1)}, bf16[2,600,768...) custom-call(bf16[2,600,768]{2,1,0:T(8,128)(2,1)} %tok_ref.3, bf16[768,1536]{1,0:T(8,128)(2,1)} %bitcast.123, ...), custom_call_target="tpu_custom_call" | custom-call | flops 13094092800 | bytes 31457280 | tf_op jit(solution)/shard_map/attention_forward/pallas_call | solution.py:103
  140.9 1.2 copy-done.1
  142.1 1.2 copy-done.2
  144.0 65.1 %feed_forward.1 = (f32[1200,768]{1,0:T(8,128)}, bf16[1200,768]{1,0:T(8,128)(2,1)}, f32[1200,768]{1,0:T(8,128)}, f32[8,768]{1,0:T(8,128)}, f32[8,3072]{1,0:T(8,128)}, /*index=5*/bf16[32,192,768]{2,1,0:T(8,128)(2,1)}) custom-call(s32[2]{0:T(128)} %len_ref.3, bf16[1200,768]{1,0:T(8,128)(2,1)} %bitcast.128, bf16[1200,768]{1,0:T(8,128)(2,1)} %bitcast.147, ...), custom_call_target="tpu_custom_call" | custom-call | flops 35389440000 | bytes 37748736 | tf_op jit(solution)/shard_map/feed_forward/pallas_call | solution.py:274
  209.1 14.2 %middle_backward.1 = (f32[2,600,768]{2,1,0:T(8,128)}, bf16[2,600,768]{2,1,0:T(8,128)(2,1)}, f32[2,24,600]{2,1,0:T(8,128)}, bf16[768,768]{1,0:T(8,128)(2,1)}, f32[8,768]{1,0:T(8,128)}) custom-call(s32[2]{0:T(128)} %len_ref.3, f32[2,600,768]{2,1,0:T(8,128)} %bitcast.115, f32[2,600,768]{2,1,0:T(8,128)} %bitcast.114, bf16[2,600,768]{2,1,0:T(8,128)(2,1)} %cot_ref.1, ...), custom_call_target="tpu_custom_call" | custom-call | flops 2831155200 | bytes 18874368 | tf_op jit(solution)/shard_map/middle_backward/pallas_call | solution.py:387
  223.3 61.3 %attention_backward.1 = (bf16[768,768]{1,0:T(8,128)(2,1)}, bf16[768,768]{1,0:T(8,128)(2,1)}, bf16[768,768]{1,0:T(8,128)(2,1)}, f32[2,600,768]{2,1,0:T(8,128)}, f32[8,2304]{1,0:T(8,128)}, /*index=5*/f32[8,768]{1,0:T(8,128)}) custom-call(bf16[2,600,768]{2,1,0:T(8,128)(2,1)} %copy-done.2, bf16[2,600,768]{2,1,0:T(8,128)(2,1)} %get-tuple-element.40.k_ref, ...), custom_call_target="tpu_custom_call" | custom-call | flops 30611865600 | bytes 37748736 | tf_op jit(solution)/shard_map/attention_backward/pallas_call | solution.py:526
  284.6 1.8 pad_maximum_fusion
  286.6 1.2 copy.228
  288.2 0.9 convert_reduce_fusion.1
  290.7 0.9 fusion.15
  292.2 0.9 concatenate.275
  293.1 0.8 concatenate.276
  294.0 0.8 copy.203
  294.8 1.7 copy.211
  296.5 0.8 copy.202
  297.3 1.1 reshape_squeeze.10
  298.4 0.8 copy.204
  299.3 1.7 pad_maximum_fusion.6
  300.9 2.4 concatenate.278
  303.4 1.1 fusion.1
  304.7 1.2 copy.227
  306.0 1.6 convert_add_fusion.1
  307.8 1.4 collective-permute-done.11
  309.3 1.6 convert_add_fusion
  310.9 1.3 collective-permute-start.12
  312.2 11.9 %collective-permute-done.9 = bf16[2,2,2,24,1536]{4,3,0,1,2:T(8,128)(2,1)S(1)} collective-permute-done((bf16[2,2,2,24,1536]{4,3,0,1,2:T(8,128)(2,1)S(1)}, bf16[2,2,2,24,1536]{4,3,0,1,2:T(8,128)(2,1)S(1)}, u32[]{:S(2)}, u32[]{:S(2)}) %collective-permute-start.9) | collective-permute-done | bytes 589856 | tf_op jit(solution)/shard_map/ppermute | solution.py:568
  324.3 1.5 collective-permute-start.10
  325.9 3.8 %collective-permute-done.12 = bf16[2,2,2,24,1664]{4,3,0,1,2:T(8,128)(2,1)S(1)} collective-permute-done((bf16[2,2,2,24,1664]{4,3,0,1,2:T(8,128)(2,1)S(1)}, bf16[2,2,2,24,1664]{4,3,0,1,2:T(8,128)(2,1)S(1)}, u32[]{:S(2)}, u32[]{:S(2)}) %collective-permute-start.12) | collective-permute-done | bytes 639008 | tf_op jit(solution)/shard_map/ppermute | solution.py:568
  329.8 1.5 collective-permute-start.13
  331.4 4.3 %collective-permute-done.10 = bf16[2,2,24,1536]{3,2,0,1:T(8,128)(2,1)S(1)} collective-permute-done((bf16[2,2,24,1536]{3,2,0,1:T(8,128)(2,1)S(1)}, bf16[2,2,24,1536]{3,2,0,1:T(8,128)(2,1)S(1)}, u32[]{:S(2)}, u32[]{:S(2)}) %collective-permute-start.10) | collective-permute-done | bytes 294944 | tf_op jit(solution)/shard_map/ppermute | solution.py:568
  335.8 5.2 %collective-permute-done.13 = bf16[2,2,24,1664]{3,2,0,1:T(8,128)(2,1)S(1)} collective-permute-done((bf16[2,2,24,1664]{3,2,0,1:T(8,128)(2,1)S(1)}, bf16[2,2,24,1664]{3,2,0,1:T(8,128)(2,1)S(1)}, u32[]{:S(2)}, u32[]{:S(2)}) %collective-permute-start.13) | collective-permute-done | bytes 319520 | tf_op jit(solution)/shard_map/ppermute | solution.py:568
  341.1 1.5 collective-permute-start.14
  342.7 9.3 %collective-permute-done.14 = bf16[2,24,3200]{2,1,0:T(8,128)(2,1)S(1)} collective-permute-done((bf16[2,24,3200]{2,1,0:T(8,128)(2,1)S(1)}, bf16[2,24,3200]{2,1,0:T(8,128)(2,1)S(1)}, u32[]{:S(2)}, u32[]{:S(2)}) %collective-permute-start.14) | collective-permute-done | bytes 307232 | tf_op jit(solution)/shard_map/ppermute | solution.py:568
  352.1 2.1 collective-permute-start.15
  354.2 6.8 %collective-permute-done.15 = bf16[24,3200]{1,0:T(8,128)(2,1)S(1)} collective-permute-done((bf16[24,3200]{1,0:T(8,128)(2,1)S(1)}, bf16[24,3200]{1,0:T(8,128)(2,1)S(1)}, u32[]{:S(2)}, u32[]{:S(2)}) %collective-permute-start.15) | collective-permute-done | bytes 153632 | tf_op jit(solution)/shard_map/ppermute | solution.py:568
  363.8 0.8 slice_reduce_fusion
  364.6 0.9 fusion.20
  (104 shorter events, 22.4 us)
Async XLA Ops:
  7.2 16.0 %copy-start.10 = (s32[2,600]{1,0:T(2,128)S(1)}, s32[2,600]{1,0:T(2,128)}, u32[]{:S(2)}) copy-start(s32[2,600]{1,0:T(2,128)} %param.18) | copy-start | bytes 14404
  7.2 16.9 %copy-start.11 = (s32[2]{0:T(128)S(1)}, s32[2]{0:T(128)}, u32[]{:S(2)}) copy-start(s32[2]{0:T(128)} %len_ref.3) | copy-start | bytes 28
  7.2 136.8 %all-gather.2.cloned.1.call-start = ((), (), s32[]{:S(2)}) async-start(), calls=%async_computation.1 | async-start | bytes 9732096 | tf_op jit(solution)/shard_map/all_gather | solution.py:648
  11.3 0.7 copy-start.8
  12.0 352.6 %reduce-scatter.2.cloned.1.call-start = ((), (), s32[]{:S(2)}) async-start(), calls=%async_computation.2 | async-start | bytes 9732096 | tf_op jit(solution)/shard_map/reduce_scatter | solution.py:693
  19.1 15.1 %collective-permute-start = (bf16[24,3200]{1,0:T(8,128)(2,1)S(1)}, bf16[24,3200]{1,0:T(8,128)(2,1)S(1)}, u32[]{:S(2)}, u32[]{:S(2)}) collective-permute-start(bf16[24,3200]{1,0:T(8,128)(2,1)S(1)} %get-tuple-element.86), channel_id=1, source_target_pairs={{0,16},{4,20},{8,24},{12,28},{16,0},{20,4},{24,8},{28,12},{1,17},{... | collective-permute-start | bytes 460808 | tf_op jit(solution)/shard_map/ppermute | solution.py:568
  34.4 10.4 %collective-permute-start.1 = (bf16[2,24,3200]{2,1,0:T(8,128)(2,1)S(1)}, bf16[2,24,3200]{2,1,0:T(8,128)(2,1)S(1)}, u32[]{:S(2)}, u32[]{:S(2)}) collective-permute-start(bf16[2,24,3200]{2,1,0:T(8,128)(2,1)S(1)} %maximum_select_fusion.10), channel_id=1, source_target_pairs={{0,8},{4,12},{8,0},{12,4},{16,24},{20,28},{24,16},{28,20},{1,9},{5... | collective-permute-start | bytes 921608 | tf_op jit(solution)/shard_map/ppermute | solution.py:568
  45.0 12.2 %collective-permute-start.2 = (bf16[2,2,24,1536]{3,2,1,0:T(8,128)(2,1)S(1)}, bf16[2,2,24,1536]{3,2,1,0:T(8,128)(2,1)S(1)}, u32[]{:S(2)}, u32[]{:S(2)}) collective-permute-start(bf16[2,2,24,1536]{3,2,1,0:T(8,128)(2,1)S(1)} %get-tuple-element.79), channel_id=1, source_target_pairs={{0,4},{4,0},{8,12},{12,8},{16,20},{20,16},{24,28},{28,24},{1,5},{5... | collective-permute-start | bytes 884744 | tf_op jit(solution)/shard_map/ppermute | solution.py:568
  46.7 15.8 %collective-permute-start.5 = (bf16[2,2,24,1664]{3,2,1,0:T(8,128)(2,1)S(1)}, bf16[2,2,24,1664]{3,2,1,0:T(8,128)(2,1)S(1)}, u32[]{:S(2)}, u32[]{:S(2)}) collective-permute-start(bf16[2,2,24,1664]{3,2,1,0:T(8,128)(2,1)S(1)} %get-tuple-element.76), channel_id=1, source_target_pairs={{0,2},{1,3},{2,0},{3,1},{4,6},{5,7},{6,4},{7,5},{8,10},{9,11},{10,... | collective-permute-start | bytes 958472 | tf_op jit(solution)/shard_map/ppermute | solution.py:568
  57.3 17.3 %collective-permute-start.3 = (bf16[2,2,2,24,1536]{4,3,1,0,2:T(8,128)(2,1)S(1)}, bf16[2,2,2,24,1536]{4,3,1,0,2:T(8,128)(2,1)S(1)}, u32[]{:S(2)}, u32[]{:S(2)}) collective-permute-start(bf16[2,2,2,24,1536]{4,3,1,0,2:T(8,128)(2,1)S(1)} %maximum_select_fusion.8), channel_id=1, source_target_pairs={{0,2},{1,3},{2,0},{3,1},{4,6},{5,7},{6,4},{7,5},{8,10},{9,11},{10,... | collective-permute-start | bytes 1769480 | tf_op jit(solution)/shard_map/ppermute | solution.py:568
  62.7 19.1 %collective-permute-start.6 = (bf16[2,2,2,24,1664]{4,3,2,1,0:T(8,128)(2,1)S(1)}, bf16[2,2,2,24,1664]{4,3,2,1,0:T(8,128)(2,1)S(1)}, u32[]{:S(2)}, u32[]{:S(2)}) collective-permute-start(bf16[2,2,2,24,1664]{4,3,2,1,0:T(8,128)(2,1)S(1)} %maximum_select_fusion.5), channel_id=1, source_target_pairs={{0,4},{4,0},{8,12},{12,8},{16,20},{20,16},{24,28},{28,24},{1,5},{5... | collective-permute-start | bytes 1916936 | tf_op jit(solution)/shard_map/ppermute | solution.py:568
  74.8 7.8 %collective-permute-start.4 = (bf16[2,2,2,2,24,1536]{5,4,1,0,2,3:T(8,128)(2,1)S(1)}, bf16[2,2,2,2,24,1536]{5,4,1,0,2,3:T(8,128)(2,1)S(1)}, u32[]{:S(2)}, u32[]{:S(2)}) collective-permute-start(bf16[2,2,2,2,24,1536]{5,4,1,0,2,3:T(8,128)(2,1)S(1)} %maximum_select_fusion.4), channel_id=1, source_target_pairs={{0,1},{1,0},{2,3},{3,2},{4,5},{5,4},{6,7},{7,6},{8,9},{9,8},{10,11... | collective-permute-start | bytes 3538952 | tf_op jit(solution)/shard_map/ppermute | solution.py:568
  81.9 3.1 collective-permute-start.7
  85.7 5.9 %copy-start.4 = (bf16[2,2,2,2,2,24,1664]{6,5,4,3,2,1,0:T(8,128)(2,1)}, bf16[2,2,2,2,2,24,1664]{6,5,4,3,2,1,0:T(8,128)(2,1)S(1)}, u32[]{:S(2)}) copy-start(bf16[2,2,2,2,2,24,1664]{6,5,4,3,2,1,0:T(8,128)(2,1)S(1)} %maximum_select_fusion) | copy-start | bytes 7667716
  95.1 45.8 %copy-start = (f32[16,768]{1,0:T(8,128)}, f32[16,768]{1,0:T(8,128)S(1)}, u32[]{:S(2)}) copy-start(f32[16,768]{1,0:T(8,128)S(1)} %concatenate.272.vec_ref.bias_ref) | copy-start | bytes 147460
  140.9 1.2 copy-start.1
  142.1 1.2 copy-start.2
  143.3 0.6 copy-start.3
  286.6 5.0 %copy-start.9 = (f32[8,768]{1,0:T(8,128)S(1)}, f32[8,768]{1,0:T(8,128)}, u32[]{:S(2)}) copy-start(f32[8,768]{1,0:T(8,128)} %get-tuple-element.56) | copy-start | bytes 73732
  287.8 18.2 %collective-permute-start.8 = (bf16[2,2,2,2,24,1536]{5,4,0,1,2,3:T(8,128)(2,1)}, bf16[2,2,2,2,24,1536]{5,4,0,1,2,3:T(8,128)(2,1)}, u32[]{:S(2)}, u32[]{:S(2)}) collective-permute-start(bf16[2,2,2,2,24,1536]{5,4,0,1,2,3:T(8,128)(2,1)} %bitcast.104), channel_id=1, source_target_pairs={{0,1},{1,0},{2,3},{3,2},{4,5},{5,4},{6,7},{7,6},{8,9},{9,8},{10,11... | collective-permute-start | bytes 3538952 | tf_op jit(solution)/shard_map/ppermute | solution.py:568
  294.8 8.6 %copy-start.5 = (bf16[768,768]{1,0:T(8,128)(2,1)S(1)}, bf16[768,768]{1,0:T(8,128)(2,1)}, u32[]{:S(2)}) copy-start(bf16[768,768]{1,0:T(8,128)(2,1)} %get-tuple-element.53) | copy-start | bytes 3538948
  294.8 8.6 %copy-start.6 = (bf16[768,768]{1,0:T(8,128)(2,1)S(1)}, bf16[768,768]{1,0:T(8,128)(2,1)}, u32[]{:S(2)}) copy-start(bf16[768,768]{1,0:T(8,128)(2,1)} %get-tuple-element.52) | copy-start | bytes 3538948
  305.9 3.3 collective-permute-start.11
  307.7 16.4 %collective-permute-start.9 = (bf16[2,2,2,24,1536]{4,3,0,1,2:T(8,128)(2,1)S(1)}, bf16[2,2,2,24,1536]{4,3,0,1,2:T(8,128)(2,1)S(1)}, u32[]{:S(2)}, u32[]{:S(2)}) collective-permute-start(bf16[2,2,2,24,1536]{4,3,0,1,2:T(8,128)(2,1)S(1)} %fusion.8), channel_id=1, source_target_pairs={{0,2},{1,3},{2,0},{3,1},{4,6},{5,7},{6,4},{7,5},{8,10},{9,11},{10,... | collective-permute-start | bytes 1769480 | tf_op jit(solution)/shard_map/ppermute | solution.py:568
  310.9 18.8 %collective-permute-start.12 = (bf16[2,2,2,24,1664]{4,3,0,1,2:T(8,128)(2,1)S(1)}, bf16[2,2,2,24,1664]{4,3,0,1,2:T(8,128)(2,1)S(1)}, u32[]{:S(2)}, u32[]{:S(2)}) collective-permute-start(bf16[2,2,2,24,1664]{4,3,0,1,2:T(8,128)(2,1)S(1)} %fusion.2), channel_id=1, source_target_pairs={{0,4},{4,0},{8,12},{12,8},{16,20},{20,16},{24,28},{28,24},{1,5},{5... | collective-permute-start | bytes 1916936 | tf_op jit(solution)/shard_map/ppermute | solution.py:568
  324.3 11.4 %collective-permute-start.10 = (bf16[2,2,24,1536]{3,2,0,1:T(8,128)(2,1)S(1)}, bf16[2,2,24,1536]{3,2,0,1:T(8,128)(2,1)S(1)}, u32[]{:S(2)}, u32[]{:S(2)}) collective-permute-start(bf16[2,2,24,1536]{3,2,0,1:T(8,128)(2,1)S(1)} %fusion.12), channel_id=1, source_target_pairs={{0,4},{4,0},{8,12},{12,8},{16,20},{20,16},{24,28},{28,24},{1,5},{5... | collective-permute-start | bytes 884744 | tf_op jit(solution)/shard_map/ppermute | solution.py:568
  329.8 11.2 %collective-permute-start.13 = (bf16[2,2,24,1664]{3,2,0,1:T(8,128)(2,1)S(1)}, bf16[2,2,24,1664]{3,2,0,1:T(8,128)(2,1)S(1)}, u32[]{:S(2)}, u32[]{:S(2)}) collective-permute-start(bf16[2,2,24,1664]{3,2,0,1:T(8,128)(2,1)S(1)} %fusion.9), channel_id=1, source_target_pairs={{0,2},{1,3},{2,0},{3,1},{4,6},{5,7},{6,4},{7,5},{8,10},{9,11},{10,... | collective-permute-start | bytes 958472 | tf_op jit(solution)/shard_map/ppermute | solution.py:568
  341.1 10.9 %collective-permute-start.14 = (bf16[2,24,3200]{2,1,0:T(8,128)(2,1)S(1)}, bf16[2,24,3200]{2,1,0:T(8,128)(2,1)S(1)}, u32[]{:S(2)}, u32[]{:S(2)}) collective-permute-start(bf16[2,24,3200]{2,1,0:T(8,128)(2,1)S(1)} %fusion.10), channel_id=1, source_target_pairs={{0,8},{4,12},{8,0},{12,4},{16,24},{20,28},{24,16},{28,20},{1,9},{5... | collective-permute-start | bytes 921608 | tf_op jit(solution)/shard_map/ppermute | solution.py:568
  352.1 8.9 %collective-permute-start.15 = (bf16[24,3200]{1,0:T(8,128)(2,1)S(1)}, bf16[24,3200]{1,0:T(8,128)(2,1)S(1)}, u32[]{:S(2)}, u32[]{:S(2)}) collective-permute-start(bf16[24,3200]{1,0:T(8,128)(2,1)S(1)} %fusion.14), channel_id=1, source_target_pairs={{0,16},{4,20},{8,24},{12,28},{16,0},{20,4},{24,8},{28,12},{1,17},{... | collective-permute-start | bytes 460808 | tf_op jit(solution)/shard_map/ppermute | solution.py:568
  364.6 1.6 copy-start.7
Sparse Core Ops, SparseCore 0:
  12.1 96.9 all-gather.1
  209.2 140.7 reduce-scatter.1
